TPU v7x, 512 devices: a whole 4x8x8 slice. The times are simulated.
512 devices in a mesh: tm: 64 (over z, x, core), pairs: 8 (over y).
Axes of the slice: x: 4, y: 8, z: 8, core: 2. Of those that a mesh axis runs over, the one named last changes fastest.
Arguments:
- records: bfloat16 [2048, 65536], P('pairs', 'tm'), may hold values from -400 to 400
- station_order: int32 [2048], replicated, may hold values from 0 to 2047, each once
- block_list: int32 [80, 2], P('pairs'), may hold values from -1 to 31, as said below
Outputs:
- correlations: bfloat16 [80, 384, 2, 4096], P('pairs', 'tm')
Inputs may be any that keep to these rules, and one draw needn't show every extreme that they name: `station_order`: each station once. `block_list`: rows k * 10 to (k + 1) * 10 - 1 belong to owner k of the pairs axis; an owner's live blocks come first and its other rows hold -1 in both columns; some owner has all 10 rows live; in a live row the second group is the first plus 0 to 3, modulo 32.
All inputs are finite; a program needn't handle non-finite values.
Results may differ from a plain program's by a relative error of at most 0.0076.
Values may be sent and summed in bfloat16 or wider, within the bound.
No kernel may reach another device: no remote copies, remote signals or barrier semaphores. Data moves between devices by JAX's collectives and lax.ppermute only.
A program may use at most 64 MiB of HBM per device.

v0:
```python
import math

import jax
import jax.numpy as jnp
import ml_dtypes
import numpy as np
from jax import lax
from jax.experimental import pallas as pl
from jax.experimental.pallas import tpu as pltpu
from jax.sharding import PartitionSpec as P

RECEIVER_TOTAL = 2048
GSIZE = 64
GROUPS = 32
SUBWIN = 16
SAMPLES = 4096
TIME = 65536
BINS = 384
FIRST_BIN = 8
BAND = 64
HALF = 64
SLOTS = 10
EPS = 1e-06

N_TIME = 64
N_OWNER = 8
QUAD = 4
SLICE = TIME // N_TIME
ROWS = RECEIVER_TOTAL // N_OWNER
PART = ROWS // QUAD
LOCAL_BINS = BINS // N_TIME
LINES = LOCAL_BINS * 2 * SUBWIN
EDGE = 128

f32 = jnp.float32
bf16 = jnp.bfloat16
NT = (((1,), (1,)), ((), ()))


def quarter_table():
    bins = np.arange(BINS)[:, None] + FIRST_BIN
    phase = (bins * np.arange(SLICE)[None, :] % SAMPLES) * (2.0 * math.pi / SAMPLES)
    return np.concatenate([np.cos(phase), -np.sin(phase)]).astype(ml_dtypes.bfloat16)


def normalize_kernel(tm_ref, x_ref, left_ref, right_ref, out_ref):
    mag = jnp.concatenate(
        [jnp.abs(left_ref[...]), jnp.abs(x_ref[...]), jnp.abs(right_ref[...])], axis=1
    )
    step = 256
    span = step + 2 * EDGE
    k = lax.broadcasted_iota(jnp.int32, (span, step), 0)
    n = lax.broadcasted_iota(jnp.int32, (span, step), 1)
    near = jnp.abs(k - EDGE - n) <= HALF
    band = jnp.where(near, 1.0, 0.0).astype(bf16)
    for j in range(SLICE // step):
        sums = jnp.dot(
            mag[:, j * step : j * step + span], band, preferred_element_type=f32
        )
        position = (
            tm_ref[0] * SLICE + j * step + lax.broadcasted_iota(jnp.int32, (1, step), 1)
        )
        upper = jnp.minimum(position + HALF, TIME - 1)
        lower = jnp.maximum(position - HALF, 0)
        counts = (upper - lower + 1).astype(f32)
        values = x_ref[:, j * step : (j + 1) * step].astype(f32)
        out_ref[:, j * step : (j + 1) * step] = (values / (sums / counts + EPS)).astype(bf16)


def spectra_kernel(table_ref, y_ref, out_ref):
    p = lax.dot_general(table_ref[...], y_ref[...], NT, preferred_element_type=f32)
    re, im = p[:BINS], p[BINS:]
    f = lax.broadcasted_iota(jnp.int32, (BINS, 128), 0)
    lane = lax.broadcasted_iota(jnp.int32, (BINS, 128), 1)
    odd = (f & 1) == 1
    low = lane < PART
    u_re = jnp.where(odd, re[:, :128] - re[:, 128:], re[:, :128] + re[:, 128:])
    u_im = jnp.where(odd, im[:, :128] - im[:, 128:], im[:, :128] + im[:, 128:])
    sign = jnp.where((f & 3) < 2, 1.0, -1.0)
    v_re = sign * jnp.where(odd, u_im, u_re)
    v_im = sign * jnp.where(odd, -u_re, u_im)
    raw = jnp.where(low, u_re, v_im) + pltpu.roll(jnp.where(low, u_im, v_re), PART, 1)
    for m in range(BINS // BAND):
        block = raw[m * BAND : (m + 1) * BAND]
        power = jnp.sum(block * block, axis=0, keepdims=True)
        power = jnp.broadcast_to(power, (8, 128))
        power = power + pltpu.roll(power, PART, 1)
        level = jnp.sqrt(power / BAND + EPS)
        out_ref[m * BAND : (m + 1) * BAND] = (block / level[:1]).astype(bf16)


def arrange_kernel(x_ref, out_ref):
    o = lax.broadcasted_iota(jnp.int32, (BINS, BINS), 0)
    i = lax.broadcasted_iota(jnp.int32, (BINS, BINS), 1)
    per = LOCAL_BINS * SUBWIN
    source = (o % SUBWIN) * (QUAD * LOCAL_BINS) + (o // per) * LOCAL_BINS + (o % per) // SUBWIN
    pick = jnp.where(i == source, 1.0, 0.0).astype(bf16)
    z = jnp.dot(pick, x_ref[...], preferred_element_type=f32)
    low = lax.broadcasted_iota(jnp.int32, (per, 128), 1) < PART
    for h in range(QUAD // 2):
        first = z[2 * h * per : (2 * h + 1) * per]
        second = z[(2 * h + 1) * per : (2 * h + 2) * per]
        parts = (
            jnp.where(low, first, pltpu.roll(second, PART, 1)).astype(bf16),
            jnp.where(low, pltpu.roll(first, PART, 1), second).astype(bf16),
        )
        for b in range(LOCAL_BINS):
            for c in range(2):
                rows = parts[c][b * SUBWIN : (b + 1) * SUBWIN]
                for n in range(N_OWNER):
                    out_ref[
                        n,
                        (2 * b + c) * SUBWIN : (2 * b + c + 1) * SUBWIN,
                        h * 128 : (h + 1) * 128,
                    ] = rows


PER_STEP = 2


def correlate_kernel(list_ref, order_ref, s_ref, out_ref, all_ref):
    step = pl.program_id(0)

    @pl.when(step == 0)
    def _():
        for n in range(N_OWNER):
            all_ref[:, n * ROWS : (n + 1) * ROWS] = s_ref[n]

    rho = lax.broadcasted_iota(jnp.int32, (GSIZE, GSIZE), 0)
    col = lax.broadcasted_iota(jnp.int32, (GSIZE, GSIZE), 1)
    even = col == (rho // 2) * 2
    uneven = col == (rho // 2) * 2 + 1
    same = col == rho
    station = lax.broadcasted_iota(jnp.int32, (3 * GSIZE, RECEIVER_TOTAL), 1)
    k = lax.broadcasted_iota(jnp.int32, (LINES, LINES), 0)
    n = lax.broadcasted_iota(jnp.int32, (LINES, LINES), 1)
    turn = jnp.where(k == (n ^ SUBWIN), jnp.where((n & SUBWIN) == 0, -1.0, 1.0), 0.0).astype(bf16)
    imag_row = (lax.broadcasted_iota(jnp.int32, (2 * GSIZE, LINES), 0) & 1) == 1
    bin_of = lax.broadcasted_iota(jnp.int32, (GSIZE, 128), 1) // (2 * SUBWIN)

    for b in range(PER_STEP):
        slot = step * PER_STEP + b
        first, second = list_ref[slot, 0], list_ref[slot, 1]
        scale = jnp.where(first >= 0, 1.0 / SUBWIN, 0.0)
        members_a = order_ref[pl.ds(jnp.maximum(first, 0), 1), :]
        members_b = order_ref[pl.ds(jnp.maximum(second, 0), 1), :]
        wanted = jnp.concatenate(
            [
                jnp.sum(jnp.where(even, members_a, 0), axis=1, keepdims=True),
                jnp.sum(jnp.where(uneven, members_a, 0), axis=1, keepdims=True),
                jnp.sum(jnp.where(same, members_b, 0), axis=1, keepdims=True),
            ],
            axis=0,
        )
        pick = jnp.where(station == wanted, 1.0, 0.0).astype(bf16)
        g = lax.dot_general(pick, all_ref[...], NT, preferred_element_type=f32).astype(bf16)
        a = g[: 2 * GSIZE]
        turned = jnp.dot(a, turn, preferred_element_type=f32)
        a = jnp.where(imag_row, turned, a.astype(f32)).astype(bf16)
        right = g[2 * GSIZE :]
        pad = jnp.zeros((GSIZE, 64), bf16)
        zero = jnp.zeros((GSIZE, 128), bf16)
        sides = (
            (a[:GSIZE, :128], a[GSIZE:, :128], right[:, :128], 0, 4),
            (
                jnp.concatenate([a[:GSIZE, 128:], pad], axis=1),
                jnp.concatenate([a[GSIZE:, 128:], pad], axis=1),
                jnp.concatenate([right[:, 128:], pad], axis=1),
                4,
                2,
            ),
        )
        for a_even, a_odd, r, bin0, count in sides:
            lhs = jnp.concatenate([a_even, a_odd], axis=1)
            blocks = []
            for e in range(count):
                kept = jnp.where(bin_of == e, r.astype(f32), 0.0).astype(bf16)
                blocks.append(jnp.concatenate([kept, zero], axis=1))
                blocks.append(jnp.concatenate([zero, kept], axis=1))
            rhs = jnp.concatenate(blocks, axis=0)
            c = lax.dot_general(lhs, rhs, NT, preferred_element_type=f32) * scale
            for e in range(count):
                out_ref[b, bin0 + e] = c[:, e * 128 : (e + 1) * 128].astype(bf16)


def vmem():
    return pl.BlockSpec(memory_space=pltpu.VMEM)


def smem():
    return pl.BlockSpec(memory_space=pltpu.SMEM)


PARAMS = pltpu.CompilerParams(vmem_limit_bytes=40 * 1024 * 1024)


def local(records, station_order, block_list):
    me = lax.axis_index("tm").astype(jnp.int32).reshape(1)
    left = lax.ppermute(records[:, SLICE - EDGE :], "tm", [(i, i + 1) for i in range(N_TIME - 1)])
    right = lax.ppermute(records[:, :EDGE], "tm", [(i + 1, i) for i in range(N_TIME - 1)])
    normalized = pl.pallas_call(
        normalize_kernel,
        out_shape=jax.ShapeDtypeStruct((ROWS, SLICE), bf16),
        in_specs=[smem(), vmem(), vmem(), vmem()],
        out_specs=vmem(),
        compiler_params=PARAMS,
        name="normalize",
    )(me, records, left, right)
    quads = [[QUAD * g + i for i in range(QUAD)] for g in range(N_TIME // QUAD)]
    windows = lax.all_to_all(
        normalized.reshape(QUAD, PART, SLICE), "tm", 0, 0, axis_index_groups=quads, tiled=True
    ).reshape(ROWS, SLICE)
    spectra = pl.pallas_call(
        spectra_kernel,
        out_shape=jax.ShapeDtypeStruct((BINS, 2 * PART), bf16),
        in_specs=[vmem(), vmem()],
        out_specs=vmem(),
        compiler_params=PARAMS,
        name="spectra",
    )(jnp.asarray(quarter_table()), windows)
    by_bin = lax.all_to_all(
        spectra.reshape(N_TIME, LOCAL_BINS // 2, 2, 2 * PART), "tm", 0, 0, tiled=True
    ).reshape(BINS, 2 * PART)
    copies = pl.pallas_call(
        arrange_kernel,
        out_shape=jax.ShapeDtypeStruct((N_OWNER, LINES, ROWS), bf16),
        in_specs=[vmem()],
        out_specs=vmem(),
        compiler_params=PARAMS,
        name="arrange",
    )(by_bin)
    stations = lax.all_to_all(copies, "pairs", 0, 0, tiled=True)
    out = pl.pallas_call(
        correlate_kernel,
        out_shape=jax.ShapeDtypeStruct((SLOTS, LOCAL_BINS, GSIZE, 128), bf16),
        grid=(SLOTS // PER_STEP,),
        in_specs=[smem(), vmem(), vmem()],
        out_specs=pl.BlockSpec((PER_STEP, LOCAL_BINS, GSIZE, 128), lambda i: (i, 0, 0, 0)),
        scratch_shapes=[pltpu.VMEM((LINES, RECEIVER_TOTAL), bf16)],
        compiler_params=PARAMS,
        name="correlate",
    )(block_list, station_order.reshape(GROUPS, GSIZE), stations)
    out = out.reshape(SLOTS, LOCAL_BINS, GSIZE // 2, 2, 128)
    return jnp.transpose(out, (0, 1, 3, 2, 4)).reshape(SLOTS, LOCAL_BINS, 2, GSIZE * GSIZE)


def solution(mesh):
    placed = (P("pairs", "tm"), P(), P("pairs", None))
    return jax.shard_map(
        local, mesh=mesh, in_specs=placed, out_specs=P("pairs", "tm", None, None), check_vma=False
    )
```

profile of v0, /device:TPU:1, one launch (start us, length us, event | category | flops | bytes accessed | tf_op | source)
XLA Modules:
  0.0 92.5 jit_solution(6658941998834285429)
XLA Ops:
  0.0 0.0 copy-start
  0.0 1.0 %fusion = (bf16[256,128]{1,0:T(8,128)(2,1)S(1)}, bf16[256,128]{1,0:T(8,128)(2,1)S(1)}) fusion(bf16[256,1024]{1,0:T(8,128)(2,1)} %x_ref.1), kind=kLoop, calls=%fused_computation | loop fusion | bytes 262144 | tf_op jit(solution)/shard_map/slice | solution.py:200
  1.0 8.8 %collective-permute-start.1 = (bf16[256,128]{1,0:T(8,128)(2,1)S(1)}, bf16[256,128]{1,0:T(8,128)(2,1)S(1)}, u32[]{:S(2)}, u32[]{:S(2)}) collective-permute-start(bf16[256,128]{1,0:T(8,128)(2,1)S(1)} %get-tuple-element.5), channel_id=1, source_target_pairs={{8,0},{16,8},{24,16},{32,24},{40,32},{48,40},{56,48},{64,56},{72,6... | collective-permute-start | bytes 196616 | tf_op jit(solution)/shard_map/ppermute | solution.py:200
  9.8 1.9 %collective-permute-start = (bf16[256,128]{1,0:T(8,128)(2,1)S(1)}, bf16[256,128]{1,0:T(8,128)(2,1)S(1)}, u32[]{:S(2)}, u32[]{:S(2)}) collective-permute-start(bf16[256,128]{1,0:T(8,128)(2,1)S(1)} %get-tuple-element.6), channel_id=1, source_target_pairs={{0,8},{8,16},{16,24},{24,32},{32,40},{40,48},{48,56},{56,64},{64,7... | collective-permute-start | bytes 196616 | tf_op jit(solution)/shard_map/ppermute | solution.py:199
  11.7 0.0 collective-permute-done.1.right_ref
  11.7 1.3 %collective-permute-done.left_ref = bf16[256,128]{1,0:T(8,128)(2,1)S(1)} collective-permute-done((bf16[256,128]{1,0:T(8,128)(2,1)S(1)}, bf16[256,128]{1,0:T(8,128)(2,1)S(1)}, u32[]{:S(2)}, u32[]{:S(2)}) %collective-permute-start) | collective-permute-done | bytes 65568 | tf_op jit(solution)/shard_map/ppermute | solution.py:199
  13.0 0.0 copy-start.1
  13.0 1.0 %copy-done.1 = bf16[256,1024]{1,0:T(8,128)(2,1)S(1)} copy-done((bf16[256,1024]{1,0:T(8,128)(2,1)S(1)}, bf16[256,1024]{1,0:T(8,128)(2,1)}, u32[]{:S(2)}) %copy-start.1) | copy-done | bytes 524312
  14.1 0.5 normalize.1
  14.6 11.6 %all_to_all.15 = bf16[4,64,1024]{2,1,0:T(8,128)(2,1)S(1)} all-to-all(bf16[4,64,1024]{2,1,0:T(8,128)(2,1)S(1)} %bitcast.10), channel_id=1, replica_groups={{0,8,16,24},{32,40,48,56},{64,72,80,88},{96,104,112,120},{128,136,144,1..., dimensions={0} | all-to-all | bytes 1048576 | tf_op jit(solution)/shard_map/all_to_all | solution.py:210
  26.2 0.0 copy-done
  26.2 0.8 spectra.1
  27.0 0.0 copy-start.3
  27.0 0.0 copy-start.2
  27.0 22.4 %all_to_all.16 = bf16[64,3,2,128]{3,2,1,0:T(2,128)(2,1)S(1)} all-to-all(bf16[64,3,2,128]{3,2,1,0:T(2,128)(2,1)S(1)} %bitcast.12), channel_id=1, replica_groups=mesh['tm'=64,'pairs'=8] {'tm'}, dimensions={0} | all-to-all | bytes 196608 | tf_op jit(solution)/shard_map/all_to_all | solution.py:221
  49.4 1.4 %arrange.1 = bf16[8,192,256]{2,1,0:T(8,128)(2,1)} custom-call(bf16[384,128]{1,0:T(8,128)(2,1)S(1)} %bitcast.13), custom_call_target="tpu_custom_call" | custom-call | tf_op jit(solution)/shard_map/arrange/pallas_call | solution.py:224
  50.8 6.8 %all-to-all-start.2 = ((bf16[8,192,256]{2,1,0:T(8,128)(2,1)}), bf16[8,192,256]{2,1,0:T(8,128)(2,1)S(1)}, u32[]{:S(2)}, u32[]{:S(2)}) async-start(bf16[8,192,256]{2,1,0:T(8,128)(2,1)} %arrange.1), calls=%async_computation.2 | async-start | bytes 1572864 | tf_op jit(solution)/shard_map/all_to_all | solution.py:232
  57.6 0.0 copy-done.3
  57.6 0.1 copy.5.list_ref
  57.7 0.0 copy-done.2
  57.7 0.1 reshape.24.order_ref
  57.8 23.4 %all-to-all-done.2.s_ref = bf16[8,192,256]{2,1,0:T(8,128)(2,1)S(1)} async-done(((bf16[8,192,256]{2,1,0:T(8,128)(2,1)}), bf16[8,192,256]{2,1,0:T(8,128)(2,1)S(1)}, u32[]{:S(2)}, u32[]{:S(2)}) %all-to-all-start.2) | async-done | bytes 786464 | tf_op jit(solution)/shard_map/all_to_all | solution.py:232
  81.2 11.3 %correlate.1 = bf16[10,6,64,128]{3,2,1,0:T(8,128)(2,1)} custom-call(s32[10,2]{1,0:T(8,128)S(1)} %copy.5.list_ref, s32[32,64]{1,0:T(8,128)S(1)} %reshape.24.order_ref, bf16[8,192,256]{2,1,0:T(8,128)(2,1)S(1)} %all-to-all-done.2.s_ref), custom_call_target="tpu_custom_call" | custom-call | tf_op jit(solution)/shard_map/correlate/pallas_call | solution.py:233
Async XLA Ops:
  0.0 26.2 %copy-start = (bf16[768,1024]{1,0:T(8,128)(2,1)S(1)}, bf16[768,1024]{1,0:T(8,128)(2,1)}, u32[]{:S(2)}) copy-start(bf16[768,1024]{1,0:T(8,128)(2,1)} %constant.8.clone.table_ref) | copy-start | bytes 4718596
  1.0 10.7 %collective-permute-start.1 = (bf16[256,128]{1,0:T(8,128)(2,1)S(1)}, bf16[256,128]{1,0:T(8,128)(2,1)S(1)}, u32[]{:S(2)}, u32[]{:S(2)}) collective-permute-start(bf16[256,128]{1,0:T(8,128)(2,1)S(1)} %get-tuple-element.5), channel_id=1, source_target_pairs={{8,0},{16,8},{24,16},{32,24},{40,32},{48,40},{56,48},{64,56},{72,6... | collective-permute-start | bytes 196616 | tf_op jit(solution)/shard_map/ppermute | solution.py:200
  9.8 3.2 %collective-permute-start = (bf16[256,128]{1,0:T(8,128)(2,1)S(1)}, bf16[256,128]{1,0:T(8,128)(2,1)S(1)}, u32[]{:S(2)}, u32[]{:S(2)}) collective-permute-start(bf16[256,128]{1,0:T(8,128)(2,1)S(1)} %get-tuple-element.6), channel_id=1, source_target_pairs={{0,8},{8,16},{16,24},{24,32},{32,40},{40,48},{48,56},{56,64},{64,7... | collective-permute-start | bytes 196616 | tf_op jit(solution)/shard_map/ppermute | solution.py:199
  13.0 1.0 %copy-start.1 = (bf16[256,1024]{1,0:T(8,128)(2,1)S(1)}, bf16[256,1024]{1,0:T(8,128)(2,1)}, u32[]{:S(2)}) copy-start(bf16[256,1024]{1,0:T(8,128)(2,1)} %x_ref.1) | copy-start | bytes 1572868
  27.0 30.6 %copy-start.3 = (s32[10,2]{0,1:T(2,128)S(1)}, s32[10,2]{0,1:T(2,128)}, u32[]{:S(2)}) copy-start(s32[10,2]{0,1:T(2,128)} %param.6) | copy-start | bytes 244
  27.0 30.7 %copy-start.2 = (s32[2048]{0:T(1024)S(1)}, s32[2048]{0:T(1024)}, u32[]{:S(2)}) copy-start(s32[2048]{0:T(1024)} %param.5) | copy-start | bytes 24580
  50.8 30.4 %all-to-all-start.2 = ((bf16[8,192,256]{2,1,0:T(8,128)(2,1)}), bf16[8,192,256]{2,1,0:T(8,128)(2,1)S(1)}, u32[]{:S(2)}, u32[]{:S(2)}) async-start(bf16[8,192,256]{2,1,0:T(8,128)(2,1)} %arrange.1), calls=%async_computation.2 | async-start | bytes 1572864 | tf_op jit(solution)/shard_map/all_to_all | solution.py:232
where the time goes:
time: 92.9 us; the launch traced here: 92.5 us
  blocking collectives  34 us (37%)
  waiting for transfers between devices  24.7 us (27%)
  starting transfers between devices  17.5 us (19%)
  Pallas kernels  14 us (15%)
  local copies, waits for them, and re-layouts  2.22 us (2%)
    all_to_all x1, waiting for transfers between devices, local(): stations = lax.all_to_all(copies, 'pairs', 0, 0, tiled=True)  23.4 us
    all_to_all x1, blocking collectives, local(): lax.all_to_all(spectra.reshape(N_TIME, LOCAL_BINS // 2, 2, 2 * PART), 'tm...  22.4 us
    all_to_all x1, blocking collectives, local(): lax.all_to_all(normalized.reshape(QUAD, PART, SLICE), 'tm', 0, 0, axis_in...  11.6 us
    pallas_call x1, Pallas kernels, local(): pl.pallas_call(correlate_kernel, out_shape=jax.ShapeDtypeStruct((SLOTS, L...  11.3 us
    ppermute x1, starting transfers between devices, local(): lax.ppermute(records[:, :EDGE], 'tm', [(i + 1, i) for i in range(N_TIME -...  8.79 us
    all_to_all x1, starting transfers between devices, local(): stations = lax.all_to_all(copies, 'pairs', 0, 0, tiled=True)  6.82 us
    ppermute x1, starting transfers between devices, local(): lax.ppermute(records[:, SLICE - EDGE:], 'tm', [(i, i + 1) for i in range(...  1.92 us
  transfers between devices with their start and end apart: 3, of which 2 were waited for; matrix products, arithmetic and copies ran while one was open for 0% of the time, Pallas kernels for 0%

commit v1 on v0

v1 whole, which is shorter than its diff:
```python
import math

import jax
import jax.numpy as jnp
import ml_dtypes
import numpy as np
from jax import lax
from jax.experimental import pallas as pl
from jax.experimental.pallas import tpu as pltpu
from jax.sharding import PartitionSpec as P

RECEIVER_TOTAL = 2048
GSIZE = 64
GROUPS = 32
SUBWIN = 16
SAMPLES = 4096
TIME = 65536
BINS = 384
FIRST_BIN = 8
BAND = 64
HALF = 64
SLOTS = 10
EPS = 1e-06

N_TIME = 64
N_OWNER = 8
QUAD = 4
SLICE = TIME // N_TIME
ROWS = RECEIVER_TOTAL // N_OWNER
PART = ROWS // QUAD
LOCAL_BINS = BINS // N_TIME
LINES = LOCAL_BINS * 2 * SUBWIN
EDGE = 128

f32 = jnp.float32
bf16 = jnp.bfloat16
NT = (((1,), (1,)), ((), ()))


def quarter_table():
    bins = np.arange(BINS)[:, None] + FIRST_BIN
    phase = (bins * np.arange(SLICE)[None, :] % SAMPLES) * (2.0 * math.pi / SAMPLES)
    return np.concatenate([np.cos(phase), -np.sin(phase)]).astype(ml_dtypes.bfloat16)


def band_matrix(span, step):
    k = lax.broadcasted_iota(jnp.int32, (span, step), 0)
    n = lax.broadcasted_iota(jnp.int32, (span, step), 1)
    return jnp.where(jnp.abs(k - EDGE - n) <= HALF, 1.0, 0.0).astype(bf16)


def normalize_inner_kernel(x_ref, out_ref):
    step = 256
    band = band_matrix(step + 2 * EDGE, step)
    for j in range((SLICE - 2 * EDGE) // step):
        mag = jnp.abs(x_ref[:, j * step : (j + 1) * step + 2 * EDGE])
        sums = jnp.dot(mag, band, preferred_element_type=f32)
        values = x_ref[:, j * step + EDGE : (j + 1) * step + EDGE].astype(f32)
        level = sums / (2 * HALF + 1)
        out_ref[:, j * step : (j + 1) * step] = (values / (level + EPS)).astype(bf16)


def normalize_edges_kernel(tm_ref, x_ref, left_ref, right_ref, inner_ref, out_ref):
    band = band_matrix(3 * EDGE, EDGE)
    me = tm_ref[0]
    out_ref[:, EDGE : SLICE - EDGE] = inner_ref[...]
    left = jnp.abs(left_ref[...].astype(f32)) * jnp.where(me > 0, 1.0, 0.0)
    right = jnp.abs(right_ref[...].astype(f32)) * jnp.where(me < N_TIME - 1, 1.0, 0.0)
    for start, mag in (
        (0, jnp.concatenate([left.astype(bf16), jnp.abs(x_ref[:, : 2 * EDGE])], axis=1)),
        (
            SLICE - EDGE,
            jnp.concatenate([jnp.abs(x_ref[:, SLICE - 2 * EDGE :]), right.astype(bf16)], axis=1),
        ),
    ):
        sums = jnp.dot(mag, band, preferred_element_type=f32)
        position = me * SLICE + start + lax.broadcasted_iota(jnp.int32, (1, EDGE), 1)
        upper = jnp.minimum(position + HALF, TIME - 1)
        lower = jnp.maximum(position - HALF, 0)
        counts = (upper - lower + 1).astype(f32)
        values = x_ref[:, start : start + EDGE].astype(f32)
        out_ref[:, start : start + EDGE] = (values / (sums / counts + EPS)).astype(bf16)


def spectra_kernel(table_ref, y_ref, out_ref):
    p = lax.dot_general(table_ref[...], y_ref[...], NT, preferred_element_type=f32)
    re, im = p[:BINS], p[BINS:]
    f = lax.broadcasted_iota(jnp.int32, (BINS, 128), 0)
    lane = lax.broadcasted_iota(jnp.int32, (BINS, 128), 1)
    odd = (f & 1) == 1
    low = lane < PART
    u_re = jnp.where(odd, re[:, :128] - re[:, 128:], re[:, :128] + re[:, 128:])
    u_im = jnp.where(odd, im[:, :128] - im[:, 128:], im[:, :128] + im[:, 128:])
    sign = jnp.where((f & 3) < 2, 1.0, -1.0)
    v_re = sign * jnp.where(odd, u_im, u_re)
    v_im = sign * jnp.where(odd, -u_re, u_im)
    raw = jnp.where(low, u_re, v_im) + pltpu.roll(jnp.where(low, u_im, v_re), PART, 1)
    for m in range(BINS // BAND):
        block = raw[m * BAND : (m + 1) * BAND]
        power = jnp.sum(block * block, axis=0, keepdims=True)
        power = jnp.broadcast_to(power, (8, 128))
        power = power + pltpu.roll(power, PART, 1)
        level = jnp.sqrt(power / BAND + EPS)
        out_ref[m * BAND : (m + 1) * BAND] = (block / level[:1]).astype(bf16)


def arrange_kernel(x_ref, out_ref):
    o = lax.broadcasted_iota(jnp.int32, (BINS, BINS), 0)
    i = lax.broadcasted_iota(jnp.int32, (BINS, BINS), 1)
    per = LOCAL_BINS * SUBWIN
    source = (o % SUBWIN) * (QUAD * LOCAL_BINS) + (o // per) * LOCAL_BINS + (o % per) // SUBWIN
    pick = jnp.where(i == source, 1.0, 0.0).astype(bf16)
    z = jnp.dot(pick, x_ref[...], preferred_element_type=f32)
    low = lax.broadcasted_iota(jnp.int32, (per, 128), 1) < PART
    for h in range(QUAD // 2):
        first = z[2 * h * per : (2 * h + 1) * per]
        second = z[(2 * h + 1) * per : (2 * h + 2) * per]
        real = jnp.where(low, first, pltpu.roll(second, PART, 1))
        imag = jnp.where(low, pltpu.roll(first, PART, 1), second)
        lines = []
        for e in range(LOCAL_BINS):
            lines += [part[e * SUBWIN : (e + 1) * SUBWIN] for part in (real, imag)]
        stations = jnp.concatenate(lines, axis=0).T.astype(bf16)
        out_ref[h * 128 : (h + 1) * 128] = stations[:, :128]
        out_ref[ROWS:, h * 64 : (h + 1) * 64] = stations[:, 128:]


def correlate_kernel(list_ref, order_ref, s_ref, out_ref, main_ref, tail_ref, gm_ref, gt_ref):
    for n in range(N_OWNER):
        block = s_ref[n * BINS : (n + 1) * BINS].astype(f32)
        main_ref[n * ROWS : (n + 1) * ROWS] = block[:ROWS]
        tail_ref[n * ROWS : n * ROWS + 128] = block[ROWS:]
        tail_ref[n * ROWS + 128 : (n + 1) * ROWS] = pltpu.roll(block[ROWS:], 64, 1)

    rights = SLOTS * 2 * GSIZE
    for b in range(SLOTS):
        base = jnp.maximum(list_ref[b, 0], 0) * GSIZE
        base_right = jnp.maximum(list_ref[b, 1], 0) * GSIZE
        for i in range(0, GSIZE, 8):
            ids = [order_ref[base + i + u] for u in range(8)]
            ids_right = [order_ref[base_right + i + u] for u in range(8)]
            for source, g_ref in ((main_ref, gm_ref), (tail_ref, gt_ref)):
                rows = [source[pl.ds(station, 1), :] for station in ids]
                for parity in range(2):
                    at = b * 2 * GSIZE + parity * GSIZE + i
                    twice = [rows[u - u % 2 + parity] for u in range(8)]
                    g_ref[at : at + 8, :] = jnp.concatenate(twice, axis=0)
                at = rights + b * GSIZE + i
                g_ref[at : at + 8, :] = jnp.concatenate(
                    [source[pl.ds(station, 1), :] for station in ids_right], axis=0
                )

    k = lax.broadcasted_iota(jnp.int32, (128, 128), 0)
    n = lax.broadcasted_iota(jnp.int32, (128, 128), 1)
    turn = jnp.where(k == (n ^ SUBWIN), jnp.where((n & SUBWIN) == 0, -1.0, 1.0), 0.0).astype(bf16)
    imag_row = (lax.broadcasted_iota(jnp.int32, (rights, 128), 0) & 1) == 1
    lefts = []
    for g_ref in (gm_ref, gt_ref):
        plain = g_ref[:rights]
        turned = jnp.dot(plain.astype(bf16), turn, preferred_element_type=f32)
        lefts.append(jnp.where(imag_row, turned, plain).astype(bf16))
    bin_of = lax.broadcasted_iota(jnp.int32, (GSIZE, 128), 1) // (2 * SUBWIN)
    zero = jnp.zeros((GSIZE, 128), bf16)
    for b in range(SLOTS):
        scale = jnp.where(list_ref[b, 0] >= 0, 1.0 / SUBWIN, 0.0)
        for a, g_ref, bin0, count in ((lefts[0], gm_ref, 0, 4), (lefts[1], gt_ref, 4, 2)):
            at = b * 2 * GSIZE
            lhs = jnp.concatenate(
                [a[at : at + GSIZE], a[at + GSIZE : at + 2 * GSIZE]], axis=1
            )
            r = g_ref[rights + b * GSIZE : rights + (b + 1) * GSIZE]
            blocks = []
            for e in range(count):
                kept = jnp.where(bin_of == e, r, 0.0).astype(bf16)
                blocks.append(jnp.concatenate([kept, zero], axis=1))
                blocks.append(jnp.concatenate([zero, kept], axis=1))
            rhs = jnp.concatenate(blocks, axis=0)
            c = lax.dot_general(lhs, rhs, NT, preferred_element_type=f32) * scale
            for e in range(count):
                out_ref[b, bin0 + e] = c[:, e * 128 : (e + 1) * 128].astype(bf16)


def vmem():
    return pl.BlockSpec(memory_space=pltpu.VMEM)


def smem():
    return pl.BlockSpec(memory_space=pltpu.SMEM)


PARAMS = pltpu.CompilerParams(vmem_limit_bytes=40 * 1024 * 1024)


def correlate(block_list, station_order, stations):
    return pl.pallas_call(
        correlate_kernel,
        out_shape=jax.ShapeDtypeStruct((SLOTS, LOCAL_BINS, GSIZE, 128), bf16),
        in_specs=[smem(), smem(), vmem()],
        out_specs=vmem(),
        scratch_shapes=[
            pltpu.VMEM((RECEIVER_TOTAL, 128), f32),
            pltpu.VMEM((RECEIVER_TOTAL, 128), f32),
            pltpu.VMEM((SLOTS * 3 * GSIZE, 128), f32),
            pltpu.VMEM((SLOTS * 3 * GSIZE, 128), f32),
        ],
        compiler_params=PARAMS,
        name="correlate",
    )(block_list, station_order, stations)


def local(records, station_order, block_list):
    me = lax.axis_index("tm").astype(jnp.int32).reshape(1)
    up = [(i, (i + 1) % N_TIME) for i in range(N_TIME)]
    left = lax.ppermute(records[:, SLICE - EDGE :], "tm", up)
    right = lax.ppermute(records[:, :EDGE], "tm", [(j, i) for i, j in up])
    inner = pl.pallas_call(
        normalize_inner_kernel,
        out_shape=jax.ShapeDtypeStruct((ROWS, SLICE - 2 * EDGE), bf16),
        in_specs=[vmem()],
        out_specs=vmem(),
        compiler_params=PARAMS,
        cost_estimate=pl.CostEstimate(
            flops=2 * ROWS * (SLICE - 2 * EDGE) * 512,
            bytes_accessed=4 * ROWS * SLICE,
            transcendentals=0,
        ),
        name="normalize_inner",
    )(records)
    normalized = pl.pallas_call(
        normalize_edges_kernel,
        out_shape=jax.ShapeDtypeStruct((ROWS, SLICE), bf16),
        in_specs=[smem(), vmem(), vmem(), vmem(), vmem()],
        out_specs=vmem(),
        compiler_params=PARAMS,
        name="normalize_edges",
    )(me, records, left, right, inner)
    quads = [[QUAD * g + i for i in range(QUAD)] for g in range(N_TIME // QUAD)]
    windows = lax.all_to_all(
        normalized.reshape(QUAD, PART, SLICE), "tm", 0, 0, axis_index_groups=quads, tiled=True
    ).reshape(ROWS, SLICE)
    spectra = pl.pallas_call(
        spectra_kernel,
        out_shape=jax.ShapeDtypeStruct((BINS, 2 * PART), bf16),
        in_specs=[vmem(), vmem()],
        out_specs=vmem(),
        compiler_params=PARAMS,
        name="spectra",
    )(jnp.asarray(quarter_table()), windows)
    by_bin = lax.all_to_all(
        spectra.reshape(N_TIME, LOCAL_BINS // 2, 2, 2 * PART), "tm", 0, 0, tiled=True
    ).reshape(BINS, 2 * PART)
    mine = pl.pallas_call(
        arrange_kernel,
        out_shape=jax.ShapeDtypeStruct((BINS, 128), bf16),
        in_specs=[vmem()],
        out_specs=vmem(),
        compiler_params=PARAMS,
        name="arrange",
    )(by_bin)
    stations = lax.all_gather(mine, "pairs", axis=0, tiled=True)
    out = correlate(block_list, station_order, stations)
    out = out.reshape(SLOTS, LOCAL_BINS, GSIZE // 2, 2, 128)
    return jnp.transpose(out, (0, 1, 3, 2, 4)).reshape(SLOTS, LOCAL_BINS, 2, GSIZE * GSIZE)


def solution(mesh):
    placed = (P("pairs", "tm"), P(), P("pairs", None))
    return jax.shard_map(
        local, mesh=mesh, in_specs=placed, out_specs=P("pairs", "tm", None, None), check_vma=False
    )
```

time: 92.9 us -> 83.2 us (0.90)
  the two profiles are of different devices: /device:TPU:1 before, /device:TPU:16 now
where the time goes in v1:
time: 83.2 us; the launch traced here: 82.8 us
  blocking collectives  38.4 us (46%)
  starting transfers between devices  19.1 us (23%)
  waiting for transfers between devices  15.9 us (19%)
  Pallas kernels  7.25 us (9%)
  local copies, waits for them, and re-layouts  2.03 us (2%)
    all_gather x1, blocking collectives, local(): stations = lax.all_gather(mine, 'pairs', axis=0, tiled=True)  27.2 us
    ppermute x1, starting transfers between devices, local(): right = lax.ppermute(records[:, :EDGE], 'tm', [(j, i) for i, j in up])  12.6 us
    all_to_all x1, blocking collectives, local(): lax.all_to_all(normalized.reshape(QUAD, PART, SLICE), 'tm', 0, 0, axis_in...  11.2 us
    all_to_all x1, waiting for transfers between devices, local(): lax.all_to_all(spectra.reshape(N_TIME, LOCAL_BINS // 2, 2, 2 * PART), 'tm...  10.4 us
    ppermute x1, waiting for transfers between devices, local(): left = lax.ppermute(records[:, SLICE - EDGE:], 'tm', up)  5.48 us
    all_to_all x1, starting transfers between devices, local(): lax.all_to_all(spectra.reshape(N_TIME, LOCAL_BINS // 2, 2, 2 * PART), 'tm...  4.62 us
    pallas_call x1, Pallas kernels, correlate(): pl.pallas_call(correlate_kernel, out_shape=jax.ShapeDtypeStruct((SLOTS, L...  4.48 us
    ppermute x1, starting transfers between devices, local(): left = lax.ppermute(records[:, SLICE - EDGE:], 'tm', up)  1.92 us
  transfers between devices with their start and end apart: 3, of which 2 were waited for; matrix products, arithmetic and copies ran while one was open for 0% of the time, Pallas kernels for 1%

profile of v1, /device:TPU:16, one launch (start us, length us, event | category | flops | bytes accessed | tf_op | source)
XLA Modules:
  0.0 82.8 jit_solution(8949458872899191504)
XLA Ops:
  0.0 0.9 %fusion = (bf16[256,128]{1,0:T(8,128)(2,1)S(1)}, bf16[256,128]{1,0:T(8,128)(2,1)S(1)}) fusion(bf16[256,1024]{1,0:T(8,128)(2,1)} %x_ref.3), kind=kLoop, calls=%fused_computation | loop fusion | bytes 262144 | tf_op jit(solution)/shard_map/slice | solution.py:215
  0.9 12.6 %collective-permute-start.1 = (bf16[256,128]{1,0:T(8,128)(2,1)S(1)}, bf16[256,128]{1,0:T(8,128)(2,1)S(1)}, u32[]{:S(2)}, u32[]{:S(2)}) collective-permute-start(bf16[256,128]{1,0:T(8,128)(2,1)S(1)} %get-tuple-element.5), channel_id=1, source_target_pairs={{8,0},{16,8},{24,16},{32,24},{40,32},{48,40},{56,48},{64,56},{72,6... | collective-permute-start | bytes 196616 | tf_op jit(solution)/shard_map/ppermute | solution.py:215
  13.5 1.9 %collective-permute-start = (bf16[256,128]{1,0:T(8,128)(2,1)S(1)}, bf16[256,128]{1,0:T(8,128)(2,1)S(1)}, u32[]{:S(2)}, u32[]{:S(2)}) collective-permute-start(bf16[256,128]{1,0:T(8,128)(2,1)S(1)} %get-tuple-element.6), channel_id=1, source_target_pairs={{0,8},{8,16},{16,24},{24,32},{32,40},{40,48},{48,56},{56,64},{64,7... | collective-permute-start | bytes 196616 | tf_op jit(solution)/shard_map/ppermute | solution.py:214
  15.4 0.0 copy-start
  15.4 1.0 %copy-done = bf16[256,1024]{1,0:T(8,128)(2,1)S(1)} copy-done((bf16[256,1024]{1,0:T(8,128)(2,1)S(1)}, bf16[256,1024]{1,0:T(8,128)(2,1)}, u32[]{:S(2)}) %copy-start) | copy-done | bytes 524312
  16.5 0.0 copy-start.1
  16.5 0.4 normalize_inner.1.inner_ref
  16.9 0.0 collective-permute-done.1.right_ref
  16.9 5.5 %collective-permute-done.left_ref = bf16[256,128]{1,0:T(8,128)(2,1)S(1)} collective-permute-done((bf16[256,128]{1,0:T(8,128)(2,1)S(1)}, bf16[256,128]{1,0:T(8,128)(2,1)S(1)}, u32[]{:S(2)}, u32[]{:S(2)}) %collective-permute-start) | collective-permute-done | bytes 65568 | tf_op jit(solution)/shard_map/ppermute | solution.py:214
  22.4 0.3 normalize_edges.1
  22.7 0.0 copy-start.3
  22.7 11.2 %all_to_all.10 = bf16[4,64,1024]{2,1,0:T(8,128)(2,1)S(1)} all-to-all(bf16[4,64,1024]{2,1,0:T(8,128)(2,1)S(1)} %bitcast.10), channel_id=1, replica_groups={{0,8,16,24},{32,40,48,56},{64,72,80,88},{96,104,112,120},{128,136,144,1..., dimensions={0} | all-to-all | bytes 1048576 | tf_op jit(solution)/shard_map/all_to_all | solution.py:238
  33.9 0.0 copy-done.1
  33.9 0.0 copy-start.2
  33.9 1.4 %spectra.1 = bf16[384,128]{1,0:T(8,128)(2,1)} custom-call(bf16[768,1024]{1,0:T(8,128)(2,1)S(1)} %copy-done.1, bf16[256,1024]{1,0:T(8,128)(2,1)S(1)} %bitcast.11), custom_call_target="tpu_custom_call" | custom-call | tf_op jit(solution)/shard_map/spectra/pallas_call | solution.py:241
  35.4 4.6 %all-to-all-start.1 = ((bf16[64,3,2,128]{3,2,1,0:T(2,128)(2,1)}), bf16[64,3,2,128]{3,2,1,0:T(2,128)(2,1)S(1)}, u32[]{:S(2)}, u32[]{:S(2)}) async-start(bf16[64,3,2,128]{3,2,1,0:T(2,128)(2,1)} %bitcast.3), calls=%async_computation.1 | async-start | bytes 196608 | tf_op jit(solution)/shard_map/all_to_all | solution.py:249
  40.0 0.0 copy-done.3
  40.0 0.1 copy.5.list_ref
  40.1 10.4 %all-to-all-done.1 = bf16[64,3,2,128]{3,2,1,0:T(2,128)(2,1)S(1)} async-done(((bf16[64,3,2,128]{3,2,1,0:T(2,128)(2,1)}), bf16[64,3,2,128]{3,2,1,0:T(2,128)(2,1)S(1)}, u32[]{:S(2)}, u32[]{:S(2)}) %all-to-all-start.1) | async-done | bytes 98336 | tf_op jit(solution)/shard_map/all_to_all | solution.py:249
  50.6 0.6 arrange.1
  51.2 27.2 %all_gather.3.s_ref = bf16[3072,128]{1,0:T(8,128)(2,1)S(1)} all-gather(bf16[384,128]{1,0:T(8,128)(2,1)S(1)} %arrange.1), channel_id=1, replica_groups=mesh['tm'=64,'pairs'=8] {'pairs'}, dimensions={0}, use_global_device_ids=true | all-gather | bytes 884736 | tf_op jit(solution)/shard_map/all_gather | solution.py:260
  78.4 0.0 copy-done.2
  78.4 4.5 %correlate.1 = bf16[10,6,64,128]{3,2,1,0:T(8,128)(2,1)} custom-call(s32[10,2]{1,0:T(8,128)S(1)} %copy.5.list_ref, s32[2048]{0:T(1024)S(1)} %copy-done.2, bf16[3072,128]{1,0:T(8,128)(2,1)S(1)} %all_gather.3.s_ref), custom_call_target="tpu_custom_call" | custom-call | tf_op jit(solution)/shard_map/correlate/pallas_call | solution.py:195
Async XLA Ops:
  0.9 16.0 %collective-permute-start.1 = (bf16[256,128]{1,0:T(8,128)(2,1)S(1)}, bf16[256,128]{1,0:T(8,128)(2,1)S(1)}, u32[]{:S(2)}, u32[]{:S(2)}) collective-permute-start(bf16[256,128]{1,0:T(8,128)(2,1)S(1)} %get-tuple-element.5), channel_id=1, source_target_pairs={{8,0},{16,8},{24,16},{32,24},{40,32},{48,40},{56,48},{64,56},{72,6... | collective-permute-start | bytes 196616 | tf_op jit(solution)/shard_map/ppermute | solution.py:215
  13.5 8.9 %collective-permute-start = (bf16[256,128]{1,0:T(8,128)(2,1)S(1)}, bf16[256,128]{1,0:T(8,128)(2,1)S(1)}, u32[]{:S(2)}, u32[]{:S(2)}) collective-permute-start(bf16[256,128]{1,0:T(8,128)(2,1)S(1)} %get-tuple-element.6), channel_id=1, source_target_pairs={{0,8},{8,16},{16,24},{24,32},{32,40},{40,48},{48,56},{56,64},{64,7... | collective-permute-start | bytes 196616 | tf_op jit(solution)/shard_map/ppermute | solution.py:214
  15.4 1.0 %copy-start = (bf16[256,1024]{1,0:T(8,128)(2,1)S(1)}, bf16[256,1024]{1,0:T(8,128)(2,1)}, u32[]{:S(2)}) copy-start(bf16[256,1024]{1,0:T(8,128)(2,1)} %x_ref.3) | copy-start | bytes 1572868
  16.5 17.5 %copy-start.1 = (bf16[768,1024]{1,0:T(8,128)(2,1)S(1)}, bf16[768,1024]{1,0:T(8,128)(2,1)}, u32[]{:S(2)}) copy-start(bf16[768,1024]{1,0:T(8,128)(2,1)} %constant.8.clone.table_ref) | copy-start | bytes 4718596
  22.7 17.3 %copy-start.3 = (s32[10,2]{0,1:T(2,128)S(1)}, s32[10,2]{0,1:T(2,128)}, u32[]{:S(2)}) copy-start(s32[10,2]{0,1:T(2,128)} %param.6) | copy-start | bytes 244
  33.9 44.4 %copy-start.2 = (s32[2048]{0:T(1024)S(1)}, s32[2048]{0:T(1024)}, u32[]{:S(2)}) copy-start(s32[2048]{0:T(1024)} %order_ref.1) | copy-start | bytes 24580
  35.4 15.2 %all-to-all-start.1 = ((bf16[64,3,2,128]{3,2,1,0:T(2,128)(2,1)}), bf16[64,3,2,128]{3,2,1,0:T(2,128)(2,1)S(1)}, u32[]{:S(2)}, u32[]{:S(2)}) async-start(bf16[64,3,2,128]{3,2,1,0:T(2,128)(2,1)} %bitcast.3), calls=%async_computation.1 | async-start | bytes 196608 | tf_op jit(solution)/shard_map/all_to_all | solution.py:249

commit v2 on v1

--- a/solution.py
+++ b/solution.py
@@ -49,7 +49,11 @@
     return jnp.where(jnp.abs(k - EDGE - n) <= HALF, 1.0, 0.0).astype(bf16)
 
 
-def normalize_inner_kernel(x_ref, out_ref):
+def normalize_inner_kernel(x_ref, up_ref, down_ref, ends_ref, out_ref):
+    up_ref[...] = x_ref[:, SLICE - EDGE :]
+    down_ref[...] = x_ref[:, :EDGE]
+    ends_ref[:, : 2 * EDGE] = x_ref[:, : 2 * EDGE]
+    ends_ref[:, 2 * EDGE :] = x_ref[:, SLICE - 2 * EDGE :]
     step = 256
     band = band_matrix(step + 2 * EDGE, step)
     for j in range((SLICE - 2 * EDGE) // step):
@@ -60,26 +64,25 @@
         out_ref[:, j * step : (j + 1) * step] = (values / (level + EPS)).astype(bf16)
 
 
-def normalize_edges_kernel(tm_ref, x_ref, left_ref, right_ref, inner_ref, out_ref):
+def normalize_edges_kernel(tm_ref, ends_ref, left_ref, right_ref, inner_ref, out_ref):
     band = band_matrix(3 * EDGE, EDGE)
     me = tm_ref[0]
     out_ref[:, EDGE : SLICE - EDGE] = inner_ref[...]
     left = jnp.abs(left_ref[...].astype(f32)) * jnp.where(me > 0, 1.0, 0.0)
     right = jnp.abs(right_ref[...].astype(f32)) * jnp.where(me < N_TIME - 1, 1.0, 0.0)
-    for start, mag in (
-        (0, jnp.concatenate([left.astype(bf16), jnp.abs(x_ref[:, : 2 * EDGE])], axis=1)),
-        (
-            SLICE - EDGE,
-            jnp.concatenate([jnp.abs(x_ref[:, SLICE - 2 * EDGE :]), right.astype(bf16)], axis=1),
-        ),
+    head, tail = ends_ref[:, : 2 * EDGE], ends_ref[:, 2 * EDGE :]
+    for start, values, mag in (
+        (0, head[:, :EDGE], jnp.concatenate([left.astype(bf16), jnp.abs(head)], axis=1)),
+        (SLICE - EDGE, tail[:, EDGE:], jnp.concatenate([jnp.abs(tail), right.astype(bf16)], axis=1)),
     ):
         sums = jnp.dot(mag, band, preferred_element_type=f32)
         position = me * SLICE + start + lax.broadcasted_iota(jnp.int32, (1, EDGE), 1)
         upper = jnp.minimum(position + HALF, TIME - 1)
         lower = jnp.maximum(position - HALF, 0)
         counts = (upper - lower + 1).astype(f32)
-        values = x_ref[:, start : start + EDGE].astype(f32)
-        out_ref[:, start : start + EDGE] = (values / (sums / counts + EPS)).astype(bf16)
+        out_ref[:, start : start + EDGE] = (
+            values.astype(f32) / (sums / counts + EPS)
+        ).astype(bf16)
 
 
 def spectra_kernel(table_ref, y_ref, out_ref):
@@ -125,7 +128,9 @@
         out_ref[ROWS:, h * 64 : (h + 1) * 64] = stations[:, 128:]
 
 
-def correlate_kernel(list_ref, order_ref, s_ref, out_ref, main_ref, tail_ref, gm_ref, gt_ref):
+def correlate_kernel(
+    list_ref, order_ref, s_ref, out_hbm, main_ref, tail_ref, gm_ref, gt_ref, out_ref, sems
+):
     for n in range(N_OWNER):
         block = s_ref[n * BINS : (n + 1) * BINS].astype(f32)
         main_ref[n * ROWS : (n + 1) * ROWS] = block[:ROWS]
@@ -134,8 +139,8 @@
 
     rights = SLOTS * 2 * GSIZE
     for b in range(SLOTS):
-        base = jnp.maximum(list_ref[b, 0], 0) * GSIZE
-        base_right = jnp.maximum(list_ref[b, 1], 0) * GSIZE
+        base = jnp.maximum(list_ref[0, b], 0) * GSIZE
+        base_right = jnp.maximum(list_ref[1, b], 0) * GSIZE
         for i in range(0, GSIZE, 8):
             ids = [order_ref[base + i + u] for u in range(8)]
             ids_right = [order_ref[base_right + i + u] for u in range(8)]
@@ -161,8 +166,9 @@
         lefts.append(jnp.where(imag_row, turned, plain).astype(bf16))
     bin_of = lax.broadcasted_iota(jnp.int32, (GSIZE, 128), 1) // (2 * SUBWIN)
     zero = jnp.zeros((GSIZE, 128), bf16)
+    copies = []
     for b in range(SLOTS):
-        scale = jnp.where(list_ref[b, 0] >= 0, 1.0 / SUBWIN, 0.0)
+        scale = jnp.where(list_ref[0, b] >= 0, 1.0 / SUBWIN, 0.0)
         for a, g_ref, bin0, count in ((lefts[0], gm_ref, 0, 4), (lefts[1], gt_ref, 4, 2)):
             at = b * 2 * GSIZE
             lhs = jnp.concatenate(
@@ -178,6 +184,10 @@
             c = lax.dot_general(lhs, rhs, NT, preferred_element_type=f32) * scale
             for e in range(count):
                 out_ref[b, bin0 + e] = c[:, e * 128 : (e + 1) * 128].astype(bf16)
+        copies.append(pltpu.make_async_copy(out_ref.at[b], out_hbm.at[b], sems.at[b]))
+        copies[-1].start()
+    for copy in copies:
+        copy.wait()
 
 
 def vmem():
@@ -196,36 +206,38 @@
         correlate_kernel,
         out_shape=jax.ShapeDtypeStruct((SLOTS, LOCAL_BINS, GSIZE, 128), bf16),
         in_specs=[smem(), smem(), vmem()],
-        out_specs=vmem(),
+        out_specs=pl.BlockSpec(memory_space=pltpu.HBM),
         scratch_shapes=[
             pltpu.VMEM((RECEIVER_TOTAL, 128), f32),
             pltpu.VMEM((RECEIVER_TOTAL, 128), f32),
             pltpu.VMEM((SLOTS * 3 * GSIZE, 128), f32),
             pltpu.VMEM((SLOTS * 3 * GSIZE, 128), f32),
+            pltpu.VMEM((SLOTS, LOCAL_BINS, GSIZE, 128), bf16),
+            pltpu.SemaphoreType.DMA((SLOTS,)),
         ],
         compiler_params=PARAMS,
         name="correlate",
-    )(block_list, station_order, stations)
+    )(block_list.T, station_order, stations)
 
 
 def local(records, station_order, block_list):
     me = lax.axis_index("tm").astype(jnp.int32).reshape(1)
     up = [(i, (i + 1) % N_TIME) for i in range(N_TIME)]
-    left = lax.ppermute(records[:, SLICE - EDGE :], "tm", up)
-    right = lax.ppermute(records[:, :EDGE], "tm", [(j, i) for i, j in up])
-    inner = pl.pallas_call(
+    last, first, ends, inner = pl.pallas_call(
         normalize_inner_kernel,
-        out_shape=jax.ShapeDtypeStruct((ROWS, SLICE - 2 * EDGE), bf16),
+        out_shape=[
+            jax.ShapeDtypeStruct((ROWS, EDGE), bf16),
+            jax.ShapeDtypeStruct((ROWS, EDGE), bf16),
+            jax.ShapeDtypeStruct((ROWS, 4 * EDGE), bf16),
+            jax.ShapeDtypeStruct((ROWS, SLICE - 2 * EDGE), bf16),
+        ],
         in_specs=[vmem()],
-        out_specs=vmem(),
-        compiler_params=PARAMS,
-        cost_estimate=pl.CostEstimate(
-            flops=2 * ROWS * (SLICE - 2 * EDGE) * 512,
-            bytes_accessed=4 * ROWS * SLICE,
-            transcendentals=0,
-        ),
+        out_specs=[vmem()] * 4,
+        compiler_params=PARAMS,
         name="normalize_inner",
     )(records)
+    left = lax.ppermute(last, "tm", up)
+    right = lax.ppermute(first, "tm", [(j, i) for i, j in up])
     normalized = pl.pallas_call(
         normalize_edges_kernel,
         out_shape=jax.ShapeDtypeStruct((ROWS, SLICE), bf16),
@@ -233,7 +245,7 @@
         out_specs=vmem(),
         compiler_params=PARAMS,
         name="normalize_edges",
-    )(me, records, left, right, inner)
+    )(me, ends, left, right, inner)
     quads = [[QUAD * g + i for i in range(QUAD)] for g in range(N_TIME // QUAD)]
     windows = lax.all_to_all(
         normalized.reshape(QUAD, PART, SLICE), "tm", 0, 0, axis_index_groups=quads, tiled=True

time: 83.2 us -> 81.1 us (0.975)
  blocking collectives: 38.4 us -> 57 us
  waiting for transfers between devices: 15.9 us -> 1.87 us
  starting transfers between devices: 19.1 us -> 14.5 us
  Pallas kernels: 7.25 us -> 6.31 us
  local copies, waits for them, and re-layouts: 2.03 us -> 1.17 us
    all_to_all x0 -> x1, blocking collectives: none -> 18.5 us  [local(): lax.all_to_all(spectra.reshape(N_TIME, LOCAL_BINS // 2, 2, 2 * PART), 'tm...]
    all_to_all x1 -> x0, waiting for transfers between devices: 10.4 us -> none  [local(): lax.all_to_all(spectra.reshape(N_TIME, LOCAL_BINS // 2, 2, 2 * PART), 'tm...]
    all_to_all x1 -> x0, starting transfers between devices: 4.62 us -> none  [local(): lax.all_to_all(spectra.reshape(N_TIME, LOCAL_BINS // 2, 2, 2 * PART), 'tm...]
    ppermute x2, waiting for transfers between devices: 5.48 us -> 1.87 us  [the longest x1 1.87 us: local(): right = lax.ppermute(first, 'tm', [(j, i) for i, j in up])]
    slice x1 -> x0, local copies, waits for them, and re-layouts: 0.88 us -> none  [local(): right = lax.ppermute(records[:, :EDGE], 'tm', [(j, i) for i, j in up])]
  transfers between devices with their start and end apart: 3 -> 2, of which waited for: 2 -> 1; matrix products, arithmetic and copies ran while one was open for 0% -> 0% of each run, Pallas kernels for 1% -> 0%
where the time goes in v2:
time: 81.1 us; the launch traced here: 80.9 us
  blocking collectives  57 us (70%)
  starting transfers between devices  14.5 us (18%)
  Pallas kernels  6.31 us (8%)
  waiting for transfers between devices  1.87 us (2%)
  local copies, waits for them, and re-layouts  1.17 us (1%)
    all_gather x1, blocking collectives, local(): stations = lax.all_gather(mine, 'pairs', axis=0, tiled=True)  27.2 us
    all_to_all x1, blocking collectives, local(): lax.all_to_all(spectra.reshape(N_TIME, LOCAL_BINS // 2, 2, 2 * PART), 'tm...  18.5 us
    ppermute x1, starting transfers between devices, local(): right = lax.ppermute(first, 'tm', [(j, i) for i, j in up])  12.6 us
    all_to_all x1, blocking collectives, local(): lax.all_to_all(normalized.reshape(QUAD, PART, SLICE), 'tm', 0, 0, axis_in...  11.2 us
    pallas_call x1, Pallas kernels, correlate(): pl.pallas_call(correlate_kernel, out_shape=jax.ShapeDtypeStruct((SLOTS, L...  4.16 us
    ppermute x1, starting transfers between devices, local(): left = lax.ppermute(last, 'tm', up)  1.92 us
    ppermute x1, waiting for transfers between devices, local(): right = lax.ppermute(first, 'tm', [(j, i) for i, j in up])  1.87 us
  transfers between devices with their start and end apart: 2, of which 1 were waited for; matrix products, arithmetic and copies ran while one was open for 0% of the time, Pallas kernels for 0%

profile of v2, /device:TPU:16, one launch (start us, length us, event | category | flops | bytes accessed | tf_op | source)
XLA Modules:
  0.0 80.9 jit_solution(15942386270214464838)
XLA Ops:
  0.0 0.0 copy-start
  0.0 0.0 copy-start.1
  0.0 1.2 %copy-done.1 = bf16[256,1024]{1,0:T(8,128)(2,1)S(1)} copy-done((bf16[256,1024]{1,0:T(8,128)(2,1)S(1)}, bf16[256,1024]{1,0:T(8,128)(2,1)}, u32[]{:S(2)}) %copy-start.1) | copy-done | bytes 524312
  1.2 0.4 normalize_inner.1
  1.6 1.9 %collective-permute-start = (bf16[256,128]{1,0:T(8,128)(2,1)S(1)}, bf16[256,128]{1,0:T(8,128)(2,1)S(1)}, u32[]{:S(2)}, u32[]{:S(2)}) collective-permute-start(bf16[256,128]{1,0:T(8,128)(2,1)S(1)} %get-tuple-element.10), channel_id=1, source_target_pairs={{0,8},{8,16},{16,24},{24,32},{32,40},{40,48},{48,56},{56,64},{64,7... | collective-permute-start | bytes 196616 | tf_op jit(solution)/shard_map/ppermute | solution.py:239
  3.5 12.6 %collective-permute-start.1 = (bf16[256,128]{1,0:T(8,128)(2,1)S(1)}, bf16[256,128]{1,0:T(8,128)(2,1)S(1)}, u32[]{:S(2)}, u32[]{:S(2)}) collective-permute-start(bf16[256,128]{1,0:T(8,128)(2,1)S(1)} %get-tuple-element.11), channel_id=1, source_target_pairs={{8,0},{16,8},{24,16},{32,24},{40,32},{48,40},{56,48},{64,56},{72,6... | collective-permute-start | bytes 196616 | tf_op jit(solution)/shard_map/ppermute | solution.py:240
  16.1 0.0 collective-permute-done.left_ref
  16.1 1.9 %collective-permute-done.1.right_ref = bf16[256,128]{1,0:T(8,128)(2,1)S(1)} collective-permute-done((bf16[256,128]{1,0:T(8,128)(2,1)S(1)}, bf16[256,128]{1,0:T(8,128)(2,1)S(1)}, u32[]{:S(2)}, u32[]{:S(2)}) %collective-permute-start.1) | collective-permute-done | bytes 65568 | tf_op jit(solution)/shard_map/ppermute | solution.py:240
  18.0 0.3 normalize_edges.1
  18.3 11.2 %all_to_all.10 = bf16[4,64,1024]{2,1,0:T(8,128)(2,1)S(1)} all-to-all(bf16[4,64,1024]{2,1,0:T(8,128)(2,1)S(1)} %bitcast.11), channel_id=1, replica_groups={{0,8,16,24},{32,40,48,56},{64,72,80,88},{96,104,112,120},{128,136,144,1..., dimensions={0} | all-to-all | bytes 1048576 | tf_op jit(solution)/shard_map/all_to_all | solution.py:250
  29.6 0.0 copy-done
  29.6 0.0 copy-start.2
  29.6 0.0 copy-start.3
  29.6 0.8 spectra.1
  30.4 18.5 %all_to_all.11 = bf16[64,3,2,128]{3,2,1,0:T(2,128)(2,1)S(1)} all-to-all(bf16[64,3,2,128]{3,2,1,0:T(2,128)(2,1)S(1)} %bitcast.13), channel_id=1, replica_groups=mesh['tm'=64,'pairs'=8] {'tm'}, dimensions={0} | all-to-all | bytes 196608 | tf_op jit(solution)/shard_map/all_to_all | solution.py:261
  48.9 0.6 arrange.1
  49.5 27.2 %all_gather.3.s_ref = bf16[3072,128]{1,0:T(8,128)(2,1)S(1)} all-gather(bf16[384,128]{1,0:T(8,128)(2,1)S(1)} %arrange.1), channel_id=1, replica_groups=mesh['tm'=64,'pairs'=8] {'pairs'}, dimensions={0}, use_global_device_ids=true | all-gather | bytes 884736 | tf_op jit(solution)/shard_map/all_gather | solution.py:272
  76.7 0.0 copy-done.2
  76.7 0.0 copy-done.3
  76.7 4.2 %correlate.1 = bf16[10,6,64,128]{3,2,1,0:T(8,128)(2,1)} custom-call(s32[2,10]{1,0:T(2,128)S(1)} %bitcast.15, s32[2048]{0:T(1024)S(1)} %copy-done.2, bf16[3072,128]{1,0:T(8,128)(2,1)S(1)} %all_gather.3.s_ref), custom_call_target="tpu_custom_call" | custom-call | tf_op jit(solution)/shard_map/correlate/pallas_call | solution.py:205
Async XLA Ops:
  0.0 29.6 %copy-start = (bf16[768,1024]{1,0:T(8,128)(2,1)S(1)}, bf16[768,1024]{1,0:T(8,128)(2,1)}, u32[]{:S(2)}) copy-start(bf16[768,1024]{1,0:T(8,128)(2,1)} %constant.8.clone.table_ref) | copy-start | bytes 4718596
  0.0 1.2 %copy-start.1 = (bf16[256,1024]{1,0:T(8,128)(2,1)S(1)}, bf16[256,1024]{1,0:T(8,128)(2,1)}, u32[]{:S(2)}) copy-start(bf16[256,1024]{1,0:T(8,128)(2,1)} %x_ref.1) | copy-start | bytes 1572868
  1.6 14.5 %collective-permute-start = (bf16[256,128]{1,0:T(8,128)(2,1)S(1)}, bf16[256,128]{1,0:T(8,128)(2,1)S(1)}, u32[]{:S(2)}, u32[]{:S(2)}) collective-permute-start(bf16[256,128]{1,0:T(8,128)(2,1)S(1)} %get-tuple-element.10), channel_id=1, source_target_pairs={{0,8},{8,16},{16,24},{24,32},{32,40},{40,48},{48,56},{56,64},{64,7... | collective-permute-start | bytes 196616 | tf_op jit(solution)/shard_map/ppermute | solution.py:239
  3.5 14.5 %collective-permute-start.1 = (bf16[256,128]{1,0:T(8,128)(2,1)S(1)}, bf16[256,128]{1,0:T(8,128)(2,1)S(1)}, u32[]{:S(2)}, u32[]{:S(2)}) collective-permute-start(bf16[256,128]{1,0:T(8,128)(2,1)S(1)} %get-tuple-element.11), channel_id=1, source_target_pairs={{8,0},{16,8},{24,16},{32,24},{40,32},{48,40},{56,48},{64,56},{72,6... | collective-permute-start | bytes 196616 | tf_op jit(solution)/shard_map/ppermute | solution.py:240
  29.6 47.1 %copy-start.2 = (s32[2048]{0:T(1024)S(1)}, s32[2048]{0:T(1024)}, u32[]{:S(2)}) copy-start(s32[2048]{0:T(1024)} %order_ref.1) | copy-start | bytes 24580
  29.6 47.1 %copy-start.3 = (s32[10,2]{0,1:T(2,128)S(1)}, s32[10,2]{0,1:T(2,128)}, u32[]{:S(2)}) copy-start(s32[10,2]{0,1:T(2,128)} %param.6) | copy-start | bytes 244

commit v3 on v2

--- a/solution.py
+++ b/solution.py
@@ -108,6 +108,7 @@
 
 
 def arrange_kernel(x_ref, out_ref):
+    out_ref[ROWS:] = jnp.zeros((ROWS, 128), bf16)
     o = lax.broadcasted_iota(jnp.int32, (BINS, BINS), 0)
     i = lax.broadcasted_iota(jnp.int32, (BINS, BINS), 1)
     per = LOCAL_BINS * SUBWIN
@@ -125,17 +126,32 @@
             lines += [part[e * SUBWIN : (e + 1) * SUBWIN] for part in (real, imag)]
         stations = jnp.concatenate(lines, axis=0).T.astype(bf16)
         out_ref[h * 128 : (h + 1) * 128] = stations[:, :128]
-        out_ref[ROWS:, h * 64 : (h + 1) * 64] = stations[:, 128:]
+        out_ref[ROWS + h * 128 : ROWS + (h + 1) * 128, :64] = stations[:, 128:]
 
 
 def correlate_kernel(
-    list_ref, order_ref, s_ref, out_hbm, main_ref, tail_ref, gm_ref, gt_ref, out_ref, sems
+    list_ref,
+    order_ref,
+    s_hbm,
+    out_hbm,
+    s_ref,
+    main_ref,
+    tail_ref,
+    gm_ref,
+    gt_ref,
+    out_ref,
+    in_sems,
+    sems,
 ):
-    for n in range(N_OWNER):
-        block = s_ref[n * BINS : (n + 1) * BINS].astype(f32)
-        main_ref[n * ROWS : (n + 1) * ROWS] = block[:ROWS]
-        tail_ref[n * ROWS : n * ROWS + 128] = block[ROWS:]
-        tail_ref[n * ROWS + 128 : (n + 1) * ROWS] = pltpu.roll(block[ROWS:], 64, 1)
+    loads = [
+        pltpu.make_async_copy(s_hbm.at[n], s_ref.at[n], in_sems.at[n]) for n in range(N_OWNER)
+    ]
+    for load in loads:
+        load.start()
+    for n, load in enumerate(loads):
+        load.wait()
+        main_ref[n * ROWS : (n + 1) * ROWS] = s_ref[n, :ROWS].astype(f32)
+        tail_ref[n * ROWS : (n + 1) * ROWS] = s_ref[n, ROWS:].astype(f32)
 
     rights = SLOTS * 2 * GSIZE
     for b in range(SLOTS):
@@ -205,19 +221,21 @@
     return pl.pallas_call(
         correlate_kernel,
         out_shape=jax.ShapeDtypeStruct((SLOTS, LOCAL_BINS, GSIZE, 128), bf16),
-        in_specs=[smem(), smem(), vmem()],
+        in_specs=[smem(), smem(), pl.BlockSpec(memory_space=pltpu.HBM)],
         out_specs=pl.BlockSpec(memory_space=pltpu.HBM),
         scratch_shapes=[
+            pltpu.VMEM((N_OWNER, 2 * ROWS, 128), bf16),
             pltpu.VMEM((RECEIVER_TOTAL, 128), f32),
             pltpu.VMEM((RECEIVER_TOTAL, 128), f32),
             pltpu.VMEM((SLOTS * 3 * GSIZE, 128), f32),
             pltpu.VMEM((SLOTS * 3 * GSIZE, 128), f32),
             pltpu.VMEM((SLOTS, LOCAL_BINS, GSIZE, 128), bf16),
+            pltpu.SemaphoreType.DMA((N_OWNER,)),
             pltpu.SemaphoreType.DMA((SLOTS,)),
         ],
-        compiler_params=PARAMS,
+        compiler_params=pltpu.CompilerParams(vmem_limit_bytes=60 * 1024 * 1024),
         name="correlate",
-    )(block_list.T, station_order, stations)
+    )(block_list.T, station_order, stations.reshape(N_OWNER, 2 * ROWS, 128))
 
 
 def local(records, station_order, block_list):
@@ -263,7 +281,7 @@
     ).reshape(BINS, 2 * PART)
     mine = pl.pallas_call(
         arrange_kernel,
-        out_shape=jax.ShapeDtypeStruct((BINS, 128), bf16),
+        out_shape=jax.ShapeDtypeStruct((2 * ROWS, 128), bf16),
         in_specs=[vmem()],
         out_specs=vmem(),
         compiler_params=PARAMS,

time: 81.1 us -> 105 us (1.29)
  the two profiles are of different devices: /device:TPU:16 before, /device:TPU:2 now
where the time goes in v3:
time: 105 us
  waiting for transfers between devices  38.7 us (37%)
  blocking collectives  37.7 us (36%)
  between operations  13.5 us (13%)
  Pallas kernels  7.9 us (8%)
  starting transfers between devices  5.56 us (5%)
  local copies, waits for them, and re-layouts  1.16 us (1%)
    all_gather x1, waiting for transfers between devices, local(): stations = lax.all_gather(mine, 'pairs', axis=0, tiled=True)  36.8 us
    all_to_all x1, blocking collectives, local(): lax.all_to_all(normalized.reshape(QUAD, PART, SLICE), 'tm', 0, 0, axis_in...  19.1 us
    all_to_all x1, blocking collectives, local(): lax.all_to_all(spectra.reshape(N_TIME, LOCAL_BINS // 2, 2, 2 * PART), 'tm...  18.7 us
    pallas_call x1, Pallas kernels, correlate(): pl.pallas_call(correlate_kernel, out_shape=jax.ShapeDtypeStruct((SLOTS, L...  5.18 us
    ppermute x1, starting transfers between devices, local(): right = lax.ppermute(first, 'tm', [(j, i) for i, j in up])  3.64 us
  transfers between devices with their start and end apart: 3, of which 2 were waited for; matrix products, arithmetic and copies ran while one was open for 0% of the time, Pallas kernels for 0%

profile of v3, /device:TPU:2, one launch (start us, length us, event | category | flops | bytes accessed | tf_op | source)
XLA Modules:
  0.0 104.5 jit_solution(6647033422119309770)
XLA Ops:
  6.5 0.0 copy-start
  6.5 0.0 all-gather.2.cloned.1.call-start
  6.5 0.0 copy-start.1
  6.5 1.2 %copy-done.1 = bf16[256,1024]{1,0:T(8,128)(2,1)S(1)} copy-done((bf16[256,1024]{1,0:T(8,128)(2,1)S(1)}, bf16[256,1024]{1,0:T(8,128)(2,1)}, u32[]{:S(2)}) %copy-start.1) | copy-done | bytes 524312
  7.7 0.4 normalize_inner.1
  8.1 1.9 %collective-permute-start = (bf16[256,128]{1,0:T(8,128)(2,1)S(1)}, bf16[256,128]{1,0:T(8,128)(2,1)S(1)}, u32[]{:S(2)}, u32[]{:S(2)}) collective-permute-start(bf16[256,128]{1,0:T(8,128)(2,1)S(1)} %get-tuple-element.10), channel_id=1, source_target_pairs={{0,8},{8,16},{16,24},{24,32},{32,40},{40,48},{48,56},{56,64},{64,7... | collective-permute-start | bytes 196616 | tf_op jit(solution)/shard_map/ppermute | solution.py:257
  10.1 3.6 %collective-permute-start.1 = (bf16[256,128]{1,0:T(8,128)(2,1)S(1)}, bf16[256,128]{1,0:T(8,128)(2,1)S(1)}, u32[]{:S(2)}, u32[]{:S(2)}) collective-permute-start(bf16[256,128]{1,0:T(8,128)(2,1)S(1)} %get-tuple-element.11), channel_id=1, source_target_pairs={{8,0},{16,8},{24,16},{32,24},{40,32},{48,40},{56,48},{64,56},{72,6... | collective-permute-start | bytes 196616 | tf_op jit(solution)/shard_map/ppermute | solution.py:258
  13.7 0.0 collective-permute-done.left_ref
  13.7 1.9 %collective-permute-done.1.right_ref = bf16[256,128]{1,0:T(8,128)(2,1)S(1)} collective-permute-done((bf16[256,128]{1,0:T(8,128)(2,1)S(1)}, bf16[256,128]{1,0:T(8,128)(2,1)S(1)}, u32[]{:S(2)}, u32[]{:S(2)}) %collective-permute-start.1) | collective-permute-done | bytes 65568 | tf_op jit(solution)/shard_map/ppermute | solution.py:258
  15.6 0.3 normalize_edges.1
  15.9 19.1 %all_to_all.10 = bf16[4,64,1024]{2,1,0:T(8,128)(2,1)S(1)} all-to-all(bf16[4,64,1024]{2,1,0:T(8,128)(2,1)S(1)} %bitcast.12), channel_id=1, replica_groups={{0,8,16,24},{32,40,48,56},{64,72,80,88},{96,104,112,120},{128,136,144,1..., dimensions={0} | all-to-all | bytes 1048576 | tf_op jit(solution)/shard_map/all_to_all | solution.py:268
  35.0 0.0 copy-done
  35.0 0.8 spectra.1
  35.8 18.7 %all_to_all.11 = bf16[64,3,2,128]{3,2,1,0:T(2,128)(2,1)S(1)} all-to-all(bf16[64,3,2,128]{3,2,1,0:T(2,128)(2,1)S(1)} %bitcast.14), channel_id=1, replica_groups=mesh['tm'=64,'pairs'=8] {'tm'}, dimensions={0} | all-to-all | bytes 196608 | tf_op jit(solution)/shard_map/all_to_all | solution.py:279
  54.5 1.2 %arrange.1 = bf16[512,128]{1,0:T(8,128)(2,1)} custom-call(bf16[384,128]{1,0:T(8,128)(2,1)S(1)} %bitcast.15), custom_call_target="tpu_custom_call" | custom-call | tf_op jit(solution)/shard_map/arrange/pallas_call | solution.py:282
  55.7 0.0 all-gather.2.cloned.1.call-update
  55.7 36.8 %all-gather.2.cloned.1.call-done = bf16[4096,128]{1,0:T(8,128)(2,1)} async-done(((bf16[512,128]{1,0:T(8,128)(2,1)}), bf16[4096,128]{1,0:T(8,128)(2,1)}) %all-gather.2.cloned.1.call-update) | async-done | bytes 1048592 | tf_op jit(solution)/shard_map/all_gather | solution.py:290
  92.5 5.2 %correlate.1 = bf16[10,6,64,128]{3,2,1,0:T(8,128)(2,1)} custom-call(s32[2,10]{1,0:T(2,128)} %bitcast.17, s32[2048]{0:T(1024)} %order_ref.1, bf16[8,512,128]{2,1,0:T(8,128)(2,1)} %bitcast.16), custom_call_target="tpu_custom_call" | custom-call | tf_op jit(solution)/shard_map/correlate/pallas_call | solution.py:221
Async XLA Ops:
  6.5 28.4 %copy-start = (bf16[768,1024]{1,0:T(8,128)(2,1)S(1)}, bf16[768,1024]{1,0:T(8,128)(2,1)}, u32[]{:S(2)}) copy-start(bf16[768,1024]{1,0:T(8,128)(2,1)} %constant.8.clone.table_ref) | copy-start | bytes 4718596
  6.5 86.0 %all-gather.2.cloned.1.call-start = ((), (), s32[]{:S(2)}) async-start(), calls=%async_computation.2 | async-start | bytes 1179648 | tf_op jit(solution)/shard_map/all_gather | solution.py:290
  6.5 1.2 %copy-start.1 = (bf16[256,1024]{1,0:T(8,128)(2,1)S(1)}, bf16[256,1024]{1,0:T(8,128)(2,1)}, u32[]{:S(2)}) copy-start(bf16[256,1024]{1,0:T(8,128)(2,1)} %x_ref.1) | copy-start | bytes 1572868
  8.1 5.6 %collective-permute-start = (bf16[256,128]{1,0:T(8,128)(2,1)S(1)}, bf16[256,128]{1,0:T(8,128)(2,1)S(1)}, u32[]{:S(2)}, u32[]{:S(2)}) collective-permute-start(bf16[256,128]{1,0:T(8,128)(2,1)S(1)} %get-tuple-element.10), channel_id=1, source_target_pairs={{0,8},{8,16},{16,24},{24,32},{32,40},{40,48},{48,56},{56,64},{64,7... | collective-permute-start | bytes 196616 | tf_op jit(solution)/shard_map/ppermute | solution.py:257
  10.1 5.5 %collective-permute-start.1 = (bf16[256,128]{1,0:T(8,128)(2,1)S(1)}, bf16[256,128]{1,0:T(8,128)(2,1)S(1)}, u32[]{:S(2)}, u32[]{:S(2)}) collective-permute-start(bf16[256,128]{1,0:T(8,128)(2,1)S(1)} %get-tuple-element.11), channel_id=1, source_target_pairs={{8,0},{16,8},{24,16},{32,24},{40,32},{48,40},{56,48},{64,56},{72,6... | collective-permute-start | bytes 196616 | tf_op jit(solution)/shard_map/ppermute | solution.py:258
Sparse Core Ops, SparseCore 0:
  55.8 36.6 all-gather.1

commit v4 on v2

--- a/solution.py
+++ b/solution.py
@@ -43,50 +43,47 @@
     return np.concatenate([np.cos(phase), -np.sin(phase)]).astype(ml_dtypes.bfloat16)
 
 
-def band_matrix(span, step):
+def stage_kernel(x_ref, out_ref):
+    out_ref[:, :SLICE] = x_ref[...]
+    out_ref[:, SLICE:] = jnp.zeros((ROWS, EDGE), bf16)
+
+
+def join_kernel(edge_ref, _, out_ref, sem):
+    copy = pltpu.make_async_copy(edge_ref, out_ref.at[:, SLICE:], sem)
+    copy.start()
+    copy.wait()
+
+
+def normalize(me, x, edge):
+    quarter = ROWS // QUAD
+    first, last = me == 0, me == SUBWIN - 1
+    before = edge[:quarter].astype(f32) * jnp.where(first, 0.0, 1.0)
+    after = edge[ROWS - quarter :].astype(f32) * jnp.where(last, 0.0, 1.0)
+    left = jnp.concatenate([before.astype(bf16), x[: ROWS - quarter, SLICE - EDGE :]], axis=0)
+    right = jnp.concatenate([x[quarter:, :EDGE], after.astype(bf16)], axis=0)
+    mag = jnp.abs(jnp.concatenate([left, x, right], axis=1))
+    step = 256
+    span = step + 2 * EDGE
     k = lax.broadcasted_iota(jnp.int32, (span, step), 0)
     n = lax.broadcasted_iota(jnp.int32, (span, step), 1)
-    return jnp.where(jnp.abs(k - EDGE - n) <= HALF, 1.0, 0.0).astype(bf16)
-
-
-def normalize_inner_kernel(x_ref, up_ref, down_ref, ends_ref, out_ref):
-    up_ref[...] = x_ref[:, SLICE - EDGE :]
-    down_ref[...] = x_ref[:, :EDGE]
-    ends_ref[:, : 2 * EDGE] = x_ref[:, : 2 * EDGE]
-    ends_ref[:, 2 * EDGE :] = x_ref[:, SLICE - 2 * EDGE :]
-    step = 256
-    band = band_matrix(step + 2 * EDGE, step)
-    for j in range((SLICE - 2 * EDGE) // step):
-        mag = jnp.abs(x_ref[:, j * step : (j + 1) * step + 2 * EDGE])
-        sums = jnp.dot(mag, band, preferred_element_type=f32)
-        values = x_ref[:, j * step + EDGE : (j + 1) * step + EDGE].astype(f32)
-        level = sums / (2 * HALF + 1)
-        out_ref[:, j * step : (j + 1) * step] = (values / (level + EPS)).astype(bf16)
-
-
-def normalize_edges_kernel(tm_ref, ends_ref, left_ref, right_ref, inner_ref, out_ref):
-    band = band_matrix(3 * EDGE, EDGE)
-    me = tm_ref[0]
-    out_ref[:, EDGE : SLICE - EDGE] = inner_ref[...]
-    left = jnp.abs(left_ref[...].astype(f32)) * jnp.where(me > 0, 1.0, 0.0)
-    right = jnp.abs(right_ref[...].astype(f32)) * jnp.where(me < N_TIME - 1, 1.0, 0.0)
-    head, tail = ends_ref[:, : 2 * EDGE], ends_ref[:, 2 * EDGE :]
-    for start, values, mag in (
-        (0, head[:, :EDGE], jnp.concatenate([left.astype(bf16), jnp.abs(head)], axis=1)),
-        (SLICE - EDGE, tail[:, EDGE:], jnp.concatenate([jnp.abs(tail), right.astype(bf16)], axis=1)),
-    ):
-        sums = jnp.dot(mag, band, preferred_element_type=f32)
-        position = me * SLICE + start + lax.broadcasted_iota(jnp.int32, (1, EDGE), 1)
+    band = jnp.where(jnp.abs(k - EDGE - n) <= HALF, 1.0, 0.0).astype(bf16)
+    row = lax.broadcasted_iota(jnp.int32, (ROWS, step), 0)
+    lane = lax.broadcasted_iota(jnp.int32, (ROWS, step), 1)
+    blocks = []
+    for j in range(SLICE // step):
+        sums = jnp.dot(mag[:, j * step : j * step + span], band, preferred_element_type=f32)
+        position = me * SAMPLES + (row // quarter) * SLICE + j * step + lane
         upper = jnp.minimum(position + HALF, TIME - 1)
         lower = jnp.maximum(position - HALF, 0)
         counts = (upper - lower + 1).astype(f32)
-        out_ref[:, start : start + EDGE] = (
-            values.astype(f32) / (sums / counts + EPS)
-        ).astype(bf16)
-
-
-def spectra_kernel(table_ref, y_ref, out_ref):
-    p = lax.dot_general(table_ref[...], y_ref[...], NT, preferred_element_type=f32)
+        values = x[:, j * step : (j + 1) * step].astype(f32)
+        blocks.append((values / (sums / counts + EPS)).astype(bf16))
+    return jnp.concatenate(blocks, axis=1)
+
+
+def spectra_kernel(me_ref, table_ref, x_ref, out_ref):
+    y = normalize(me_ref[0] // QUAD, x_ref[:, :SLICE], x_ref[:, SLICE:])
+    p = lax.dot_general(table_ref[...], y, NT, preferred_element_type=f32)
     re, im = p[:BINS], p[BINS:]
     f = lax.broadcasted_iota(jnp.int32, (BINS, 128), 0)
     lane = lax.broadcasted_iota(jnp.int32, (BINS, 128), 1)
@@ -221,43 +218,43 @@
 
 
 def local(records, station_order, block_list):
-    me = lax.axis_index("tm").astype(jnp.int32).reshape(1)
-    up = [(i, (i + 1) % N_TIME) for i in range(N_TIME)]
-    last, first, ends, inner = pl.pallas_call(
-        normalize_inner_kernel,
-        out_shape=[
-            jax.ShapeDtypeStruct((ROWS, EDGE), bf16),
-            jax.ShapeDtypeStruct((ROWS, EDGE), bf16),
-            jax.ShapeDtypeStruct((ROWS, 4 * EDGE), bf16),
-            jax.ShapeDtypeStruct((ROWS, SLICE - 2 * EDGE), bf16),
-        ],
+    me = lax.axis_index("tm").astype(jnp.int32)
+    facing = lax.dynamic_slice(records, (0, (me & 1) * (SLICE - EDGE)), (ROWS, EDGE))
+    swap = [(i, i + 1 if i % 2 else i - 1) for i in range(N_TIME)]
+    edge = lax.ppermute(facing, "tm", [(i, j % N_TIME) for i, j in swap])
+    staged = pl.pallas_call(
+        stage_kernel,
+        out_shape=jax.ShapeDtypeStruct((ROWS, SLICE + EDGE), bf16),
         in_specs=[vmem()],
-        out_specs=[vmem()] * 4,
-        compiler_params=PARAMS,
-        name="normalize_inner",
+        out_specs=vmem(),
+        compiler_params=PARAMS,
+        cost_estimate=pl.CostEstimate(
+            flops=2 * ROWS * SLICE * 512, bytes_accessed=4 * ROWS * SLICE, transcendentals=0
+        ),
+        name="stage",
     )(records)
-    left = lax.ppermute(last, "tm", up)
-    right = lax.ppermute(first, "tm", [(j, i) for i, j in up])
-    normalized = pl.pallas_call(
-        normalize_edges_kernel,
-        out_shape=jax.ShapeDtypeStruct((ROWS, SLICE), bf16),
-        in_specs=[smem(), vmem(), vmem(), vmem(), vmem()],
-        out_specs=vmem(),
-        compiler_params=PARAMS,
-        name="normalize_edges",
-    )(me, ends, left, right, inner)
+    extended = pl.pallas_call(
+        join_kernel,
+        out_shape=jax.ShapeDtypeStruct((ROWS, SLICE + EDGE), bf16),
+        in_specs=[pl.BlockSpec(memory_space=pl.ANY)] * 2,
+        out_specs=pl.BlockSpec(memory_space=pl.ANY),
+        scratch_shapes=[pltpu.SemaphoreType.DMA(())],
+        input_output_aliases={1: 0},
+        compiler_params=PARAMS,
+        name="join",
+    )(edge, staged)
     quads = [[QUAD * g + i for i in range(QUAD)] for g in range(N_TIME // QUAD)]
     windows = lax.all_to_all(
-        normalized.reshape(QUAD, PART, SLICE), "tm", 0, 0, axis_index_groups=quads, tiled=True
-    ).reshape(ROWS, SLICE)
+        extended.reshape(QUAD, PART, SLICE + EDGE), "tm", 0, 0, axis_index_groups=quads, tiled=True
+    ).reshape(ROWS, SLICE + EDGE)
     spectra = pl.pallas_call(
         spectra_kernel,
         out_shape=jax.ShapeDtypeStruct((BINS, 2 * PART), bf16),
-        in_specs=[vmem(), vmem()],
+        in_specs=[smem(), vmem(), vmem()],
         out_specs=vmem(),
         compiler_params=PARAMS,
         name="spectra",
-    )(jnp.asarray(quarter_table()), windows)
+    )(me.reshape(1), jnp.asarray(quarter_table()), windows)
     by_bin = lax.all_to_all(
         spectra.reshape(N_TIME, LOCAL_BINS // 2, 2, 2 * PART), "tm", 0, 0, tiled=True
     ).reshape(BINS, 2 * PART)

time: 81.1 us -> 79 us (0.974)
  starting transfers between devices: 14.5 us -> 12.7 us
  waiting for transfers between devices: 1.87 us -> 0.84 us
    ppermute x2 -> x1, starting transfers between devices: 14.5 us -> 12.7 us  [local(): edge = lax.ppermute(facing, 'tm', [(i, j % N_TIME) for i, j in swap])]
    ppermute x2 -> x1, waiting for transfers between devices: 1.87 us -> 0.84 us  [local(): edge = lax.ppermute(facing, 'tm', [(i, j % N_TIME) for i, j in swap])]
    dynamic_slice x0 -> x1, local copies, waits for them, and re-layouts: none -> 0.84 us  [local(): lax.dynamic_slice(records, (0, (me & 1) * (SLICE - EDGE)), (ROWS, EDGE))]
  transfers between devices with their start and end apart: 2 -> 1, of which waited for: 1 -> 1; matrix products, arithmetic and copies ran while one was open for 0% -> 0% of each run, Pallas kernels for 0% -> 0%
where the time goes in v4:
time: 79 us; the launch traced here: 78.7 us
  blocking collectives  56.9 us (72%)
  starting transfers between devices  12.7 us (16%)
  Pallas kernels  6.35 us (8%)
  local copies, waits for them, and re-layouts  1.89 us (2%)
  waiting for transfers between devices  0.84 us (1%)
    all_gather x1, blocking collectives, local(): stations = lax.all_gather(mine, 'pairs', axis=0, tiled=True)  27.2 us
    all_to_all x1, blocking collectives, local(): lax.all_to_all(spectra.reshape(N_TIME, LOCAL_BINS // 2, 2, 2 * PART), 'tm...  17.8 us
    ppermute x1, starting transfers between devices, local(): edge = lax.ppermute(facing, 'tm', [(i, j % N_TIME) for i, j in swap])  12.7 us
    all_to_all x1, blocking collectives, local(): lax.all_to_all(extended.reshape(QUAD, PART, SLICE + EDGE), 'tm', 0, 0, ax...  11.9 us
    pallas_call x1, Pallas kernels, correlate(): pl.pallas_call(correlate_kernel, out_shape=jax.ShapeDtypeStruct((SLOTS, L...  4.17 us
  transfers between devices with their start and end apart: 1, of which 1 were waited for; matrix products, arithmetic and copies ran while one was open for 0% of the time, Pallas kernels for 0%

profile of v4, /device:TPU:16, one launch (start us, length us, event | category | flops | bytes accessed | tf_op | source)
XLA Modules:
  0.0 78.7 jit_solution(5639165301297091265)
XLA Ops:
  0.0 0.8 %constant_dynamic-slice_fusion = bf16[256,128]{1,0:T(8,128)(2,1)S(1)} fusion(bf16[256,1024]{1,0:T(8,128)(2,1)} %x_ref.1, s32[]{:T(128)S(6)} %select_n.3), kind=kLoop, calls=%fused_computation | loop fusion | bytes 131076 | tf_op jit(solution)/shard_map/dynamic_slice | solution.py:222
  0.8 0.0 copy-start
  0.8 12.7 %collective-permute-start = (bf16[256,128]{1,0:T(8,128)(2,1)S(1)}, bf16[256,128]{1,0:T(8,128)(2,1)S(1)}, u32[]{:S(2)}, u32[]{:S(2)}) collective-permute-start(bf16[256,128]{1,0:T(8,128)(2,1)S(1)} %constant_dynamic-slice_fusion), channel_id=1, source_target_pairs={{0,504},{8,16},{16,8},{24,32},{32,24},{40,48},{48,40},{56,64},{64,... | collective-permute-start | bytes 196616 | tf_op jit(solution)/shard_map/ppermute | solution.py:224
  13.6 0.0 copy-start.1
  13.6 1.0 %copy-done.1 = bf16[256,1024]{1,0:T(8,128)(2,1)S(1)} copy-done((bf16[256,1024]{1,0:T(8,128)(2,1)S(1)}, bf16[256,1024]{1,0:T(8,128)(2,1)}, u32[]{:S(2)}) %copy-start.1) | copy-done | bytes 524312
  14.6 0.8 %collective-permute-done.edge_ref = bf16[256,128]{1,0:T(8,128)(2,1)S(1)} collective-permute-done((bf16[256,128]{1,0:T(8,128)(2,1)S(1)}, bf16[256,128]{1,0:T(8,128)(2,1)S(1)}, u32[]{:S(2)}, u32[]{:S(2)}) %collective-permute-start) | collective-permute-done | bytes 65568 | tf_op jit(solution)/shard_map/ppermute | solution.py:224
  15.5 11.9 %all_to_all.10 = bf16[4,64,1152]{2,1,0:T(8,128)(2,1)S(1)} all-to-all(bf16[4,64,1152]{2,1,0:T(8,128)(2,1)S(1)} %bitcast.11), channel_id=1, replica_groups={{0,8,16,24},{32,40,48,56},{64,72,80,88},{96,104,112,120},{128,136,144,1..., dimensions={0} | all-to-all | bytes 1179648 | tf_op jit(solution)/shard_map/all_to_all | solution.py:247
  27.5 0.0 copy-done
  27.5 0.0 copy-start.2
  27.5 0.0 copy-start.3
  27.5 1.5 %spectra.1 = bf16[384,128]{1,0:T(8,128)(2,1)S(1)} custom-call(s32[1]{0:T(128)} %bitcast.1.me_ref, bf16[768,1024]{1,0:T(8,128)(2,1)S(1)} %copy-done, bf16[256,1152]{1,0:T(8,128)(2,1)S(1)} %bitcast.12), custom_call_target="tpu_custom_call" | custom-call | tf_op jit(solution)/shard_map/spectra/pallas_call | solution.py:250
  29.0 17.8 %all_to_all.11 = bf16[64,3,2,128]{3,2,1,0:T(2,128)(2,1)S(1)} all-to-all(bf16[64,3,2,128]{3,2,1,0:T(2,128)(2,1)S(1)} %bitcast.13), channel_id=1, replica_groups=mesh['tm'=64,'pairs'=8] {'tm'}, dimensions={0} | all-to-all | bytes 196608 | tf_op jit(solution)/shard_map/all_to_all | solution.py:258
  46.8 0.6 arrange.1
  47.4 27.2 %all_gather.3.s_ref = bf16[3072,128]{1,0:T(8,128)(2,1)S(1)} all-gather(bf16[384,128]{1,0:T(8,128)(2,1)S(1)} %arrange.1), channel_id=1, replica_groups=mesh['tm'=64,'pairs'=8] {'pairs'}, dimensions={0}, use_global_device_ids=true | all-gather | bytes 884736 | tf_op jit(solution)/shard_map/all_gather | solution.py:269
  74.6 0.0 copy-done.2
  74.6 0.0 copy-done.3
  74.6 4.2 %correlate.1 = bf16[10,6,64,128]{3,2,1,0:T(8,128)(2,1)} custom-call(s32[2,10]{1,0:T(2,128)S(1)} %bitcast.15, s32[2048]{0:T(1024)S(1)} %copy-done.2, bf16[3072,128]{1,0:T(8,128)(2,1)S(1)} %all_gather.3.s_ref), custom_call_target="tpu_custom_call" | custom-call | tf_op jit(solution)/shard_map/correlate/pallas_call | solution.py:202
  (2 shorter events, 0.1 us)
Async XLA Ops:
  0.8 26.6 %copy-start = (bf16[768,1024]{1,0:T(8,128)(2,1)S(1)}, bf16[768,1024]{1,0:T(8,128)(2,1)}, u32[]{:S(2)}) copy-start(bf16[768,1024]{1,0:T(8,128)(2,1)} %constant.16.clone.table_ref) | copy-start | bytes 4718596
  0.8 14.6 %collective-permute-start = (bf16[256,128]{1,0:T(8,128)(2,1)S(1)}, bf16[256,128]{1,0:T(8,128)(2,1)S(1)}, u32[]{:S(2)}, u32[]{:S(2)}) collective-permute-start(bf16[256,128]{1,0:T(8,128)(2,1)S(1)} %constant_dynamic-slice_fusion), channel_id=1, source_target_pairs={{0,504},{8,16},{16,8},{24,32},{32,24},{40,48},{48,40},{56,64},{64,... | collective-permute-start | bytes 196616 | tf_op jit(solution)/shard_map/ppermute | solution.py:224
  13.6 1.0 %copy-start.1 = (bf16[256,1024]{1,0:T(8,128)(2,1)S(1)}, bf16[256,1024]{1,0:T(8,128)(2,1)}, u32[]{:S(2)}) copy-start(bf16[256,1024]{1,0:T(8,128)(2,1)} %x_ref.1) | copy-start | bytes 1572868
  27.5 47.1 %copy-start.2 = (s32[2048]{0:T(1024)S(1)}, s32[2048]{0:T(1024)}, u32[]{:S(2)}) copy-start(s32[2048]{0:T(1024)} %order_ref.1) | copy-start | bytes 24580
  27.5 47.1 %copy-start.3 = (s32[10,2]{0,1:T(2,128)S(1)}, s32[10,2]{0,1:T(2,128)}, u32[]{:S(2)}) copy-start(s32[10,2]{0,1:T(2,128)} %param.6) | copy-start | bytes 244

commit v5 on v4

--- a/solution.py
+++ b/solution.py
@@ -72,17 +72,19 @@
     blocks = []
     for j in range(SLICE // step):
         sums = jnp.dot(mag[:, j * step : j * step + span], band, preferred_element_type=f32)
-        position = me * SAMPLES + (row // quarter) * SLICE + j * step + lane
-        upper = jnp.minimum(position + HALF, TIME - 1)
-        lower = jnp.maximum(position - HALF, 0)
-        counts = (upper - lower + 1).astype(f32)
+        counts = 2 * HALF + 1.0
+        if j == 0 or j == SLICE // step - 1:
+            position = me * SAMPLES + (row // quarter) * SLICE + j * step + lane
+            upper = jnp.minimum(position + HALF, TIME - 1)
+            lower = jnp.maximum(position - HALF, 0)
+            counts = (upper - lower + 1).astype(f32)
         values = x[:, j * step : (j + 1) * step].astype(f32)
         blocks.append((values / (sums / counts + EPS)).astype(bf16))
     return jnp.concatenate(blocks, axis=1)
 
 
-def spectra_kernel(me_ref, table_ref, x_ref, out_ref):
-    y = normalize(me_ref[0] // QUAD, x_ref[:, :SLICE], x_ref[:, SLICE:])
+def spectra_kernel(table_ref, x_ref, out_ref):
+    y = normalize(lax.axis_index("tm") // QUAD, x_ref[:, :SLICE], x_ref[:, SLICE:])
     p = lax.dot_general(table_ref[...], y, NT, preferred_element_type=f32)
     re, im = p[:BINS], p[BINS:]
     f = lax.broadcasted_iota(jnp.int32, (BINS, 128), 0)
@@ -126,15 +128,35 @@
 
 
 def correlate_kernel(
-    list_ref, order_ref, s_ref, out_hbm, main_ref, tail_ref, gm_ref, gt_ref, out_ref, sems
+    list_any,
+    order_any,
+    s_ref,
+    out_hbm,
+    main_ref,
+    tail_ref,
+    gm_ref,
+    gt_ref,
+    out_ref,
+    order_ref,
+    order_sem,
+    list_ref,
+    list_sem,
+    sems,
 ):
+    order_copy = pltpu.make_async_copy(order_any, order_ref, order_sem)
+    order_copy.start()
+    list_copy = pltpu.make_async_copy(list_any, list_ref, list_sem)
+    list_copy.start()
     for n in range(N_OWNER):
         block = s_ref[n * BINS : (n + 1) * BINS].astype(f32)
         main_ref[n * ROWS : (n + 1) * ROWS] = block[:ROWS]
         tail_ref[n * ROWS : n * ROWS + 128] = block[ROWS:]
         tail_ref[n * ROWS + 128 : (n + 1) * ROWS] = pltpu.roll(block[ROWS:], 64, 1)
 
+    order_copy.wait()
+    list_copy.wait()
     rights = SLOTS * 2 * GSIZE
+    sub = lax.broadcasted_iota(jnp.int32, (8, 128), 0)
     for b in range(SLOTS):
         base = jnp.maximum(list_ref[0, b], 0) * GSIZE
         base_right = jnp.maximum(list_ref[1, b], 0) * GSIZE
@@ -142,15 +164,18 @@
             ids = [order_ref[base + i + u] for u in range(8)]
             ids_right = [order_ref[base_right + i + u] for u in range(8)]
             for source, g_ref in ((main_ref, gm_ref), (tail_ref, gt_ref)):
-                rows = [source[pl.ds(station, 1), :] for station in ids]
+                rows = [source[pl.ds(station, 8, stride=0), :] for station in ids]
                 for parity in range(2):
                     at = b * 2 * GSIZE + parity * GSIZE + i
-                    twice = [rows[u - u % 2 + parity] for u in range(8)]
-                    g_ref[at : at + 8, :] = jnp.concatenate(twice, axis=0)
+                    low = jnp.where(sub < 2, rows[parity], rows[2 + parity])
+                    high = jnp.where(sub < 6, rows[4 + parity], rows[6 + parity])
+                    g_ref[at : at + 8, :] = jnp.where(sub < 4, low, high)
+                rows = [source[pl.ds(station, 8, stride=0), :] for station in ids_right]
+                pairs = [jnp.where(sub % 2 == 0, rows[u], rows[u + 1]) for u in range(0, 8, 2)]
+                low = jnp.where(sub < 2, pairs[0], pairs[1])
+                high = jnp.where(sub < 6, pairs[2], pairs[3])
                 at = rights + b * GSIZE + i
-                g_ref[at : at + 8, :] = jnp.concatenate(
-                    [source[pl.ds(station, 1), :] for station in ids_right], axis=0
-                )
+                g_ref[at : at + 8, :] = jnp.where(sub < 4, low, high)
 
     k = lax.broadcasted_iota(jnp.int32, (128, 128), 0)
     n = lax.broadcasted_iota(jnp.int32, (128, 128), 1)
@@ -161,7 +186,8 @@
         plain = g_ref[:rights]
         turned = jnp.dot(plain.astype(bf16), turn, preferred_element_type=f32)
         lefts.append(jnp.where(imag_row, turned, plain).astype(bf16))
-    bin_of = lax.broadcasted_iota(jnp.int32, (GSIZE, 128), 1) // (2 * SUBWIN)
+    bin_of = (lax.broadcasted_iota(jnp.int32, (GSIZE, 256), 1) & 127) // (2 * SUBWIN)
+    keeps = [jnp.where(bin_of == e, 1.0, 0.0).astype(bf16) for e in range(4)]
     zero = jnp.zeros((GSIZE, 128), bf16)
     copies = []
     for b in range(SLOTS):
@@ -171,16 +197,14 @@
             lhs = jnp.concatenate(
                 [a[at : at + GSIZE], a[at + GSIZE : at + 2 * GSIZE]], axis=1
             )
-            r = g_ref[rights + b * GSIZE : rights + (b + 1) * GSIZE]
-            blocks = []
-            for e in range(count):
-                kept = jnp.where(bin_of == e, r, 0.0).astype(bf16)
-                blocks.append(jnp.concatenate([kept, zero], axis=1))
-                blocks.append(jnp.concatenate([zero, kept], axis=1))
-            rhs = jnp.concatenate(blocks, axis=0)
+            lhs = jnp.concatenate([lhs * keep for keep in keeps[:count]], axis=0)
+            r = g_ref[rights + b * GSIZE : rights + (b + 1) * GSIZE].astype(bf16)
+            rhs = jnp.concatenate(
+                [jnp.concatenate([r, zero], axis=1), jnp.concatenate([zero, r], axis=1)], axis=0
+            )
             c = lax.dot_general(lhs, rhs, NT, preferred_element_type=f32) * scale
             for e in range(count):
-                out_ref[b, bin0 + e] = c[:, e * 128 : (e + 1) * 128].astype(bf16)
+                out_ref[b, bin0 + e] = c[e * GSIZE : (e + 1) * GSIZE].astype(bf16)
         copies.append(pltpu.make_async_copy(out_ref.at[b], out_hbm.at[b], sems.at[b]))
         copies[-1].start()
     for copy in copies:
@@ -191,10 +215,6 @@
     return pl.BlockSpec(memory_space=pltpu.VMEM)
 
 
-def smem():
-    return pl.BlockSpec(memory_space=pltpu.SMEM)
-
-
 PARAMS = pltpu.CompilerParams(vmem_limit_bytes=40 * 1024 * 1024)
 
 
@@ -202,7 +222,7 @@
     return pl.pallas_call(
         correlate_kernel,
         out_shape=jax.ShapeDtypeStruct((SLOTS, LOCAL_BINS, GSIZE, 128), bf16),
-        in_specs=[smem(), smem(), vmem()],
+        in_specs=[pl.BlockSpec(memory_space=pl.ANY), pl.BlockSpec(memory_space=pl.ANY), vmem()],
         out_specs=pl.BlockSpec(memory_space=pltpu.HBM),
         scratch_shapes=[
             pltpu.VMEM((RECEIVER_TOTAL, 128), f32),
@@ -210,6 +230,10 @@
             pltpu.VMEM((SLOTS * 3 * GSIZE, 128), f32),
             pltpu.VMEM((SLOTS * 3 * GSIZE, 128), f32),
             pltpu.VMEM((SLOTS, LOCAL_BINS, GSIZE, 128), bf16),
+            pltpu.SMEM((RECEIVER_TOTAL,), jnp.int32),
+            pltpu.SemaphoreType.DMA(()),
+            pltpu.SMEM((2, SLOTS), jnp.int32),
+            pltpu.SemaphoreType.DMA(()),
             pltpu.SemaphoreType.DMA((SLOTS,)),
         ],
         compiler_params=PARAMS,
@@ -250,11 +274,11 @@
     spectra = pl.pallas_call(
         spectra_kernel,
         out_shape=jax.ShapeDtypeStruct((BINS, 2 * PART), bf16),
-        in_specs=[smem(), vmem(), vmem()],
+        in_specs=[vmem(), vmem()],
         out_specs=vmem(),
         compiler_params=PARAMS,
         name="spectra",
-    )(me.reshape(1), jnp.asarray(quarter_table()), windows)
+    )(jnp.asarray(quarter_table()), windows)
     by_bin = lax.all_to_all(
         spectra.reshape(N_TIME, LOCAL_BINS // 2, 2, 2 * PART), "tm", 0, 0, tiled=True
     ).reshape(BINS, 2 * PART)

time: 79 us -> 78 us (0.987)
  Pallas kernels: 6.35 us -> 5.27 us
    pallas_call x1, Pallas kernels: 4.17 us -> 3.3 us  [correlate(): pl.pallas_call(correlate_kernel, out_shape=jax.ShapeDtypeStruct((SLOTS, L...]
where the time goes in v5:
time: 78 us; the launch traced here: 77.7 us
  blocking collectives  56.9 us (73%)
  starting transfers between devices  12.7 us (16%)
  Pallas kernels  5.27 us (7%)
  local copies, waits for them, and re-layouts  1.89 us (2%)
  waiting for transfers between devices  0.84 us (1%)
    all_gather x1, blocking collectives, local(): stations = lax.all_gather(mine, 'pairs', axis=0, tiled=True)  27.2 us
    all_to_all x1, blocking collectives, local(): lax.all_to_all(spectra.reshape(N_TIME, LOCAL_BINS // 2, 2, 2 * PART), 'tm...  17.8 us
    ppermute x1, starting transfers between devices, local(): edge = lax.ppermute(facing, 'tm', [(i, j % N_TIME) for i, j in swap])  12.7 us
    all_to_all x1, blocking collectives, local(): lax.all_to_all(extended.reshape(QUAD, PART, SLICE + EDGE), 'tm', 0, 0, ax...  11.9 us
    pallas_call x1, Pallas kernels, correlate(): pl.pallas_call(correlate_kernel, out_shape=jax.ShapeDtypeStruct((SLOTS, L...  3.3 us
  transfers between devices with their start and end apart: 1, of which 1 were waited for; matrix products, arithmetic and copies ran while one was open for 0% of the time, Pallas kernels for 0%

profile of v5, /device:TPU:16, one launch (start us, length us, event | category | flops | bytes accessed | tf_op | source)
XLA Modules:
  0.0 77.7 jit_solution(13769218706762552019)
XLA Ops:
  0.0 0.8 %constant_dynamic-slice_fusion = bf16[256,128]{1,0:T(8,128)(2,1)S(1)} fusion(bf16[256,1024]{1,0:T(8,128)(2,1)} %x_ref.1, s32[]{:T(128)S(6)} %select_n.3), kind=kLoop, calls=%fused_computation | loop fusion | bytes 131076 | tf_op jit(solution)/shard_map/dynamic_slice | solution.py:246
  0.8 0.0 copy-start
  0.8 12.7 %collective-permute-start = (bf16[256,128]{1,0:T(8,128)(2,1)S(1)}, bf16[256,128]{1,0:T(8,128)(2,1)S(1)}, u32[]{:S(2)}, u32[]{:S(2)}) collective-permute-start(bf16[256,128]{1,0:T(8,128)(2,1)S(1)} %constant_dynamic-slice_fusion), channel_id=1, source_target_pairs={{0,504},{8,16},{16,8},{24,32},{32,24},{40,48},{48,40},{56,64},{64,... | collective-permute-start | bytes 196616 | tf_op jit(solution)/shard_map/ppermute | solution.py:248
  13.6 0.0 copy-start.1
  13.6 1.0 %copy-done.1 = bf16[256,1024]{1,0:T(8,128)(2,1)S(1)} copy-done((bf16[256,1024]{1,0:T(8,128)(2,1)S(1)}, bf16[256,1024]{1,0:T(8,128)(2,1)}, u32[]{:S(2)}) %copy-start.1) | copy-done | bytes 524312
  14.6 0.8 %collective-permute-done.edge_ref = bf16[256,128]{1,0:T(8,128)(2,1)S(1)} collective-permute-done((bf16[256,128]{1,0:T(8,128)(2,1)S(1)}, bf16[256,128]{1,0:T(8,128)(2,1)S(1)}, u32[]{:S(2)}, u32[]{:S(2)}) %collective-permute-start) | collective-permute-done | bytes 65568 | tf_op jit(solution)/shard_map/ppermute | solution.py:248
  15.5 11.9 %all_to_all.10 = bf16[4,64,1152]{2,1,0:T(8,128)(2,1)S(1)} all-to-all(bf16[4,64,1152]{2,1,0:T(8,128)(2,1)S(1)} %bitcast.10), channel_id=1, replica_groups={{0,8,16,24},{32,40,48,56},{64,72,80,88},{96,104,112,120},{128,136,144,1..., dimensions={0} | all-to-all | bytes 1179648 | tf_op jit(solution)/shard_map/all_to_all | solution.py:271
  27.5 0.0 copy-done
  27.5 0.0 copy-start.2
  27.5 0.0 copy-start.3
  27.5 1.3 %spectra.1 = bf16[384,128]{1,0:T(8,128)(2,1)S(1)} custom-call(bf16[768,1024]{1,0:T(8,128)(2,1)S(1)} %copy-done, bf16[256,1152]{1,0:T(8,128)(2,1)S(1)} %bitcast.11), custom_call_target="tpu_custom_call" | custom-call | tf_op jit(solution)/shard_map/spectra/pallas_call | solution.py:274
  28.8 17.8 %all_to_all.11 = bf16[64,3,2,128]{3,2,1,0:T(2,128)(2,1)S(1)} all-to-all(bf16[64,3,2,128]{3,2,1,0:T(2,128)(2,1)S(1)} %bitcast.12), channel_id=1, replica_groups=mesh['tm'=64,'pairs'=8] {'tm'}, dimensions={0} | all-to-all | bytes 196608 | tf_op jit(solution)/shard_map/all_to_all | solution.py:282
  46.6 0.6 arrange.1
  47.2 27.2 %all_gather.3.s_ref = bf16[3072,128]{1,0:T(8,128)(2,1)S(1)} all-gather(bf16[384,128]{1,0:T(8,128)(2,1)S(1)} %arrange.1), channel_id=1, replica_groups=mesh['tm'=64,'pairs'=8] {'pairs'}, dimensions={0}, use_global_device_ids=true | all-gather | bytes 884736 | tf_op jit(solution)/shard_map/all_gather | solution.py:293
  74.4 0.0 copy-done.2
  74.4 0.0 copy-done.3
  74.4 3.3 %correlate.1 = bf16[10,6,64,128]{3,2,1,0:T(8,128)(2,1)} custom-call(s32[2,10]{1,0:T(2,128)S(1)} %bitcast.14, s32[2048]{0:T(1024)S(1)} %copy-done.2, bf16[3072,128]{1,0:T(8,128)(2,1)S(1)} %all_gather.3.s_ref), custom_call_target="tpu_custom_call" | custom-call | tf_op jit(solution)/shard_map/correlate/pallas_call | solution.py:222
  (2 shorter events, 0.1 us)
Async XLA Ops:
  0.8 26.6 %copy-start = (bf16[768,1024]{1,0:T(8,128)(2,1)S(1)}, bf16[768,1024]{1,0:T(8,128)(2,1)}, u32[]{:S(2)}) copy-start(bf16[768,1024]{1,0:T(8,128)(2,1)} %constant.16.clone.table_ref) | copy-start | bytes 4718596
  0.8 14.6 %collective-permute-start = (bf16[256,128]{1,0:T(8,128)(2,1)S(1)}, bf16[256,128]{1,0:T(8,128)(2,1)S(1)}, u32[]{:S(2)}, u32[]{:S(2)}) collective-permute-start(bf16[256,128]{1,0:T(8,128)(2,1)S(1)} %constant_dynamic-slice_fusion), channel_id=1, source_target_pairs={{0,504},{8,16},{16,8},{24,32},{32,24},{40,48},{48,40},{56,64},{64,... | collective-permute-start | bytes 196616 | tf_op jit(solution)/shard_map/ppermute | solution.py:248
  13.6 1.0 %copy-start.1 = (bf16[256,1024]{1,0:T(8,128)(2,1)S(1)}, bf16[256,1024]{1,0:T(8,128)(2,1)}, u32[]{:S(2)}) copy-start(bf16[256,1024]{1,0:T(8,128)(2,1)} %x_ref.1) | copy-start | bytes 1572868
  27.5 46.9 %copy-start.2 = (s32[2048]{0:T(1024)S(1)}, s32[2048]{0:T(1024)}, u32[]{:S(2)}) copy-start(s32[2048]{0:T(1024)} %order_any.1) | copy-start | bytes 24580
  27.5 46.9 %copy-start.3 = (s32[10,2]{0,1:T(2,128)S(1)}, s32[10,2]{0,1:T(2,128)}, u32[]{:S(2)}) copy-start(s32[10,2]{0,1:T(2,128)} %param.6) | copy-start | bytes 244

commit v6 on v5

--- a/solution.py
+++ b/solution.py
@@ -43,13 +43,23 @@
     return np.concatenate([np.cos(phase), -np.sin(phase)]).astype(ml_dtypes.bfloat16)
 
 
-def stage_kernel(x_ref, out_ref):
+def stage_kernel(x_ref, facing_ref, out_ref):
     out_ref[:, :SLICE] = x_ref[...]
     out_ref[:, SLICE:] = jnp.zeros((ROWS, EDGE), bf16)
-
-
-def join_kernel(edge_ref, _, out_ref, sem):
-    copy = pltpu.make_async_copy(edge_ref, out_ref.at[:, SLICE:], sem)
+    odd = lax.axis_index("tm") % 2 == 1
+
+    @pl.when(odd)
+    def _():
+        facing_ref[...] = x_ref[:, SLICE - EDGE :]
+
+    @pl.when(jnp.logical_not(odd))
+    def _():
+        facing_ref[...] = x_ref[:, :EDGE]
+
+
+def join_kernel(edges_ref, _, out_ref, sem):
+    other = lax.axis_index("tm") % 2
+    copy = pltpu.make_async_copy(edges_ref.at[other], out_ref.at[:, SLICE:], sem)
     copy.start()
     copy.wait()
 
@@ -242,21 +252,19 @@
 
 
 def local(records, station_order, block_list):
-    me = lax.axis_index("tm").astype(jnp.int32)
-    facing = lax.dynamic_slice(records, (0, (me & 1) * (SLICE - EDGE)), (ROWS, EDGE))
-    swap = [(i, i + 1 if i % 2 else i - 1) for i in range(N_TIME)]
-    edge = lax.ppermute(facing, "tm", [(i, j % N_TIME) for i, j in swap])
-    staged = pl.pallas_call(
+    facing, staged = pl.pallas_call(
         stage_kernel,
-        out_shape=jax.ShapeDtypeStruct((ROWS, SLICE + EDGE), bf16),
+        out_shape=[
+            jax.ShapeDtypeStruct((ROWS, EDGE), bf16),
+            jax.ShapeDtypeStruct((ROWS, SLICE + EDGE), bf16),
+        ],
         in_specs=[vmem()],
-        out_specs=vmem(),
-        compiler_params=PARAMS,
-        cost_estimate=pl.CostEstimate(
-            flops=2 * ROWS * SLICE * 512, bytes_accessed=4 * ROWS * SLICE, transcendentals=0
-        ),
+        out_specs=[vmem()] * 2,
+        compiler_params=PARAMS,
         name="stage",
     )(records)
+    pairs = [[i, (i + 1) % N_TIME] for i in range(1, N_TIME, 2)]
+    edges = lax.all_gather(facing, "tm", axis_index_groups=pairs)
     extended = pl.pallas_call(
         join_kernel,
         out_shape=jax.ShapeDtypeStruct((ROWS, SLICE + EDGE), bf16),
@@ -266,7 +274,7 @@
         input_output_aliases={1: 0},
         compiler_params=PARAMS,
         name="join",
-    )(edge, staged)
+    )(edges, staged)
     quads = [[QUAD * g + i for i in range(QUAD)] for g in range(N_TIME // QUAD)]
     windows = lax.all_to_all(
         extended.reshape(QUAD, PART, SLICE + EDGE), "tm", 0, 0, axis_index_groups=quads, tiled=True

time: 78 us -> 76.9 us (0.986)
  blocking collectives: 56.9 us -> 70.2 us
  starting transfers between devices: 12.7 us -> 0 us
  waiting for transfers between devices: 0.84 us -> 0 us
    all_gather x0 -> x1, blocking collectives: none -> 13.3 us  [local(): edges = lax.all_gather(facing, 'tm', axis_index_groups=pairs)]
    ppermute x1 -> x0, starting transfers between devices: 12.7 us -> none  [local(): edge = lax.ppermute(facing, 'tm', [(i, j % N_TIME) for i, j in swap])]
    dynamic_slice x1 -> x0, local copies, waits for them, and re-layouts: 0.84 us -> none  [local(): lax.dynamic_slice(records, (0, (me & 1) * (SLICE - EDGE)), (ROWS, EDGE))]
    ppermute x1 -> x0, waiting for transfers between devices: 0.84 us -> none  [local(): edge = lax.ppermute(facing, 'tm', [(i, j % N_TIME) for i, j in swap])]
  transfers between devices with their start and end apart: 1 -> 0, of which waited for: 1 -> 0; matrix products, arithmetic and copies ran while one was open for 0% -> 0% of each run, Pallas kernels for 0% -> 0%
where the time goes in v6:
time: 76.9 us; the launch traced here: 76.7 us
  blocking collectives  70.2 us (91%)
  Pallas kernels  5.29 us (7%)
  local copies, waits for them, and re-layouts  1.17 us (2%)
    all_gather x1, blocking collectives, local(): stations = lax.all_gather(mine, 'pairs', axis=0, tiled=True)  27.2 us
    all_to_all x1, blocking collectives, local(): lax.all_to_all(spectra.reshape(N_TIME, LOCAL_BINS // 2, 2, 2 * PART), 'tm...  17.8 us
    all_gather x1, blocking collectives, local(): edges = lax.all_gather(facing, 'tm', axis_index_groups=pairs)  13.3 us
    all_to_all x1, blocking collectives, local(): lax.all_to_all(extended.reshape(QUAD, PART, SLICE + EDGE), 'tm', 0, 0, ax...  11.9 us
    pallas_call x1, Pallas kernels, correlate(): pl.pallas_call(correlate_kernel, out_shape=jax.ShapeDtypeStruct((SLOTS, L...  3.3 us

profile of v6, /device:TPU:16, one launch (start us, length us, event | category | flops | bytes accessed | tf_op | source)
XLA Modules:
  0.0 76.7 jit_solution(15068676981178831649)
XLA Ops:
  0.0 0.0 copy-start
  0.0 0.0 copy-start.1
  0.0 1.2 %copy-done.1 = bf16[256,1024]{1,0:T(8,128)(2,1)S(1)} copy-done((bf16[256,1024]{1,0:T(8,128)(2,1)S(1)}, bf16[256,1024]{1,0:T(8,128)(2,1)}, u32[]{:S(2)}) %copy-start.1) | copy-done | bytes 524312
  1.2 0.1 stage.1
  1.2 13.3 %all-gather = bf16[512,128]{1,0:T(8,128)(2,1)S(1)} all-gather(bf16[256,128]{1,0:T(8,128)(2,1)S(1)} %get-tuple-element.7), channel_id=2, replica_groups={{8,16},{24,32},{40,48},{56,64},{72,80},{88,96},{104,112},{120,128},{136..., dimensions={0}, use_global_device_ids=true | all-gather | bytes 196608 | tf_op jit(solution)/shard_map/all_gather | solution.py:267
  14.5 11.9 %all_to_all.10 = bf16[4,64,1152]{2,1,0:T(8,128)(2,1)S(1)} all-to-all(bf16[4,64,1152]{2,1,0:T(8,128)(2,1)S(1)} %bitcast.11), channel_id=1, replica_groups={{0,8,16,24},{32,40,48,56},{64,72,80,88},{96,104,112,120},{128,136,144,1..., dimensions={0} | all-to-all | bytes 1179648 | tf_op jit(solution)/shard_map/all_to_all | solution.py:279
  26.5 0.0 copy-done
  26.5 0.0 copy-start.2
  26.5 0.0 copy-start.3
  26.5 1.3 %spectra.1 = bf16[384,128]{1,0:T(8,128)(2,1)S(1)} custom-call(bf16[768,1024]{1,0:T(8,128)(2,1)S(1)} %copy-done, bf16[256,1152]{1,0:T(8,128)(2,1)S(1)} %bitcast.12), custom_call_target="tpu_custom_call" | custom-call | tf_op jit(solution)/shard_map/spectra/pallas_call | solution.py:282
  27.8 17.8 %all_to_all.11 = bf16[64,3,2,128]{3,2,1,0:T(2,128)(2,1)S(1)} all-to-all(bf16[64,3,2,128]{3,2,1,0:T(2,128)(2,1)S(1)} %bitcast.14), channel_id=1, replica_groups=mesh['tm'=64,'pairs'=8] {'tm'}, dimensions={0} | all-to-all | bytes 196608 | tf_op jit(solution)/shard_map/all_to_all | solution.py:290
  45.6 0.6 arrange.1
  46.2 27.2 %all_gather.11.s_ref = bf16[3072,128]{1,0:T(8,128)(2,1)S(1)} all-gather(bf16[384,128]{1,0:T(8,128)(2,1)S(1)} %arrange.1), channel_id=1, replica_groups=mesh['tm'=64,'pairs'=8] {'pairs'}, dimensions={0}, use_global_device_ids=true | all-gather | bytes 884736 | tf_op jit(solution)/shard_map/all_gather | solution.py:301
  73.4 0.0 copy-done.2
  73.4 0.0 copy-done.3
  73.4 3.3 %correlate.1 = bf16[10,6,64,128]{3,2,1,0:T(8,128)(2,1)} custom-call(s32[2,10]{1,0:T(2,128)S(1)} %bitcast.16, s32[2048]{0:T(1024)S(1)} %copy-done.2, bf16[3072,128]{1,0:T(8,128)(2,1)S(1)} %all_gather.11.s_ref), custom_call_target="tpu_custom_call" | custom-call | tf_op jit(solution)/shard_map/correlate/pallas_call | solution.py:232
  (1 shorter events, 0.0 us)
Async XLA Ops:
  0.0 26.5 %copy-start = (bf16[768,1024]{1,0:T(8,128)(2,1)S(1)}, bf16[768,1024]{1,0:T(8,128)(2,1)}, u32[]{:S(2)}) copy-start(bf16[768,1024]{1,0:T(8,128)(2,1)} %constant.2.clone.table_ref) | copy-start | bytes 4718596
  0.0 1.2 %copy-start.1 = (bf16[256,1024]{1,0:T(8,128)(2,1)S(1)}, bf16[256,1024]{1,0:T(8,128)(2,1)}, u32[]{:S(2)}) copy-start(bf16[256,1024]{1,0:T(8,128)(2,1)} %x_ref.1) | copy-start | bytes 1572868
  26.5 46.9 %copy-start.2 = (s32[2048]{0:T(1024)S(1)}, s32[2048]{0:T(1024)}, u32[]{:S(2)}) copy-start(s32[2048]{0:T(1024)} %order_any.1) | copy-start | bytes 24580
  26.5 46.9 %copy-start.3 = (s32[10,2]{0,1:T(2,128)S(1)}, s32[10,2]{0,1:T(2,128)}, u32[]{:S(2)}) copy-start(s32[10,2]{0,1:T(2,128)} %param.6) | copy-start | bytes 244

commit v7 on v6

--- a/solution.py
+++ b/solution.py
@@ -43,34 +43,64 @@
     return np.concatenate([np.cos(phase), -np.sin(phase)]).astype(ml_dtypes.bfloat16)
 
 
+TILES = SLICE // 128
+BODY = TILES * PART
+PACKED = PART // 2
+
+
 def stage_kernel(x_ref, facing_ref, out_ref):
-    out_ref[:, :SLICE] = x_ref[...]
-    out_ref[:, SLICE:] = jnp.zeros((ROWS, EDGE), bf16)
+    low = lax.broadcasted_iota(jnp.int32, (PACKED, 128), 1) < HALF
+
+    def pack(column, first_half):
+        edge = x_ref[:, column : column + 128].astype(f32)
+        for q in range(QUAD):
+            a = edge[q * PART : q * PART + PACKED]
+            b = edge[q * PART + PACKED : (q + 1) * PART]
+            if first_half:
+                b = pltpu.roll(b, HALF, 1)
+            else:
+                a = pltpu.roll(a, HALF, 1)
+            facing_ref[q * PACKED : (q + 1) * PACKED] = jnp.where(low, a, b).astype(bf16)
+
     odd = lax.axis_index("tm") % 2 == 1
 
     @pl.when(odd)
     def _():
-        facing_ref[...] = x_ref[:, SLICE - EDGE :]
+        pack(SLICE - 128, False)
 
     @pl.when(jnp.logical_not(odd))
     def _():
-        facing_ref[...] = x_ref[:, :EDGE]
-
-
-def join_kernel(edges_ref, _, out_ref, sem):
+        pack(0, True)
+
+    for q in range(QUAD):
+        for c in range(TILES):
+            out_ref[q, c * PART : (c + 1) * PART] = x_ref[
+                q * PART : (q + 1) * PART, c * 128 : (c + 1) * 128
+            ]
+        out_ref[q, BODY:] = jnp.zeros((PACKED, 128), bf16)
+
+
+def join_kernel(edges_ref, _, out_ref, sems):
     other = lax.axis_index("tm") % 2
-    copy = pltpu.make_async_copy(edges_ref.at[other], out_ref.at[:, SLICE:], sem)
-    copy.start()
-    copy.wait()
-
-
-def normalize(me, x, edge):
-    quarter = ROWS // QUAD
-    first, last = me == 0, me == SUBWIN - 1
-    before = edge[:quarter].astype(f32) * jnp.where(first, 0.0, 1.0)
-    after = edge[ROWS - quarter :].astype(f32) * jnp.where(last, 0.0, 1.0)
-    left = jnp.concatenate([before.astype(bf16), x[: ROWS - quarter, SLICE - EDGE :]], axis=0)
-    right = jnp.concatenate([x[quarter:, :EDGE], after.astype(bf16)], axis=0)
+    copies = [
+        pltpu.make_async_copy(
+            edges_ref.at[other, q * PACKED : (q + 1) * PACKED], out_ref.at[q, BODY:], sems.at[q]
+        )
+        for q in range(QUAD)
+    ]
+    for copy in copies:
+        copy.start()
+    for copy in copies:
+        copy.wait()
+
+
+def normalize(me, x, edge_before, edge_after):
+    before = edge_before.astype(f32) * jnp.where(me == 0, 0.0, 1.0)
+    after = edge_after.astype(f32) * jnp.where(me == SUBWIN - 1, 0.0, 1.0)
+    before = jnp.concatenate([pltpu.roll(before, HALF, 1), before], axis=0).astype(bf16)
+    after = jnp.concatenate([after, pltpu.roll(after, HALF, 1)], axis=0).astype(bf16)
+    left = jnp.concatenate([before, x[: ROWS - PART, SLICE - EDGE :]], axis=0)
+    right = jnp.concatenate([x[PART:, :EDGE], after], axis=0)
     mag = jnp.abs(jnp.concatenate([left, x, right], axis=1))
     step = 256
     span = step + 2 * EDGE
@@ -84,17 +114,22 @@
         sums = jnp.dot(mag[:, j * step : j * step + span], band, preferred_element_type=f32)
         counts = 2 * HALF + 1.0
         if j == 0 or j == SLICE // step - 1:
-            position = me * SAMPLES + (row // quarter) * SLICE + j * step + lane
+            position = me * SAMPLES + (row // PART) * SLICE + j * step + lane
             upper = jnp.minimum(position + HALF, TIME - 1)
             lower = jnp.maximum(position - HALF, 0)
             counts = (upper - lower + 1).astype(f32)
         values = x[:, j * step : (j + 1) * step].astype(f32)
-        blocks.append((values / (sums / counts + EPS)).astype(bf16))
+        blocks.append((values * counts / (sums + EPS * counts)).astype(bf16))
     return jnp.concatenate(blocks, axis=1)
 
 
 def spectra_kernel(table_ref, x_ref, out_ref):
-    y = normalize(lax.axis_index("tm") // QUAD, x_ref[:, :SLICE], x_ref[:, SLICE:])
+    columns = [
+        jnp.concatenate([x_ref[q, c * PART : (c + 1) * PART] for q in range(QUAD)], axis=0)
+        for c in range(TILES)
+    ]
+    x = jnp.concatenate(columns, axis=1)
+    y = normalize(lax.axis_index("tm") // QUAD, x, x_ref[0, BODY:], x_ref[QUAD - 1, BODY:])
     p = lax.dot_general(table_ref[...], y, NT, preferred_element_type=f32)
     re, im = p[:BINS], p[BINS:]
     f = lax.broadcasted_iota(jnp.int32, (BINS, 128), 0)
@@ -116,13 +151,14 @@
         out_ref[m * BAND : (m + 1) * BAND] = (block / level[:1]).astype(bf16)
 
 
-def arrange_kernel(x_ref, out_ref):
-    o = lax.broadcasted_iota(jnp.int32, (BINS, BINS), 0)
-    i = lax.broadcasted_iota(jnp.int32, (BINS, BINS), 1)
+def bin_rows():
+    rows = np.arange(BINS).reshape(SUBWIN, QUAD, LOCAL_BINS).transpose(1, 2, 0).reshape(-1)
+    return (np.arange(BINS)[None, :] == rows[:, None]).astype(ml_dtypes.bfloat16)
+
+
+def arrange_kernel(pick_ref, x_ref, out_ref):
     per = LOCAL_BINS * SUBWIN
-    source = (o % SUBWIN) * (QUAD * LOCAL_BINS) + (o // per) * LOCAL_BINS + (o % per) // SUBWIN
-    pick = jnp.where(i == source, 1.0, 0.0).astype(bf16)
-    z = jnp.dot(pick, x_ref[...], preferred_element_type=f32)
+    z = jnp.dot(pick_ref[...], x_ref[...], preferred_element_type=f32)
     low = lax.broadcasted_iota(jnp.int32, (per, 128), 1) < PART
     for h in range(QUAD // 2):
         first = z[2 * h * per : (2 * h + 1) * per]
@@ -255,8 +291,8 @@
     facing, staged = pl.pallas_call(
         stage_kernel,
         out_shape=[
-            jax.ShapeDtypeStruct((ROWS, EDGE), bf16),
-            jax.ShapeDtypeStruct((ROWS, SLICE + EDGE), bf16),
+            jax.ShapeDtypeStruct((QUAD * PACKED, 128), bf16),
+            jax.ShapeDtypeStruct((QUAD, BODY + PACKED, 128), bf16),
         ],
         in_specs=[vmem()],
         out_specs=[vmem()] * 2,
@@ -267,18 +303,16 @@
     edges = lax.all_gather(facing, "tm", axis_index_groups=pairs)
     extended = pl.pallas_call(
         join_kernel,
-        out_shape=jax.ShapeDtypeStruct((ROWS, SLICE + EDGE), bf16),
+        out_shape=jax.ShapeDtypeStruct((QUAD, BODY + PACKED, 128), bf16),
         in_specs=[pl.BlockSpec(memory_space=pl.ANY)] * 2,
         out_specs=pl.BlockSpec(memory_space=pl.ANY),
-        scratch_shapes=[pltpu.SemaphoreType.DMA(())],
+        scratch_shapes=[pltpu.SemaphoreType.DMA((QUAD,))],
         input_output_aliases={1: 0},
         compiler_params=PARAMS,
         name="join",
     )(edges, staged)
     quads = [[QUAD * g + i for i in range(QUAD)] for g in range(N_TIME // QUAD)]
-    windows = lax.all_to_all(
-        extended.reshape(QUAD, PART, SLICE + EDGE), "tm", 0, 0, axis_index_groups=quads, tiled=True
-    ).reshape(ROWS, SLICE + EDGE)
+    windows = lax.all_to_all(extended, "tm", 0, 0, axis_index_groups=quads, tiled=True)
     spectra = pl.pallas_call(
         spectra_kernel,
         out_shape=jax.ShapeDtypeStruct((BINS, 2 * PART), bf16),
@@ -293,11 +327,11 @@
     mine = pl.pallas_call(
         arrange_kernel,
         out_shape=jax.ShapeDtypeStruct((BINS, 128), bf16),
-        in_specs=[vmem()],
+        in_specs=[vmem()] * 2,
         out_specs=vmem(),
         compiler_params=PARAMS,
         name="arrange",
-    )(by_bin)
+    )(jnp.asarray(bin_rows()), by_bin)
     stations = lax.all_gather(mine, "pairs", axis=0, tiled=True)
     out = correlate(block_list, station_order, stations)
     out = out.reshape(SLOTS, LOCAL_BINS, GSIZE // 2, 2, 128)

time: 76.9 us -> 76.4 us (level)
  no operation moved by 1% of the time
where the time goes in v7:
time: 76.4 us; the launch traced here: 76.2 us
  blocking collectives  69.6 us (91%)
  Pallas kernels  5.36 us (7%)
  local copies, waits for them, and re-layouts  1.18 us (2%)
    all_gather x1, blocking collectives, local(): stations = lax.all_gather(mine, 'pairs', axis=0, tiled=True)  27.2 us
    all_to_all x1, blocking collectives, local(): lax.all_to_all(spectra.reshape(N_TIME, LOCAL_BINS // 2, 2, 2 * PART), 'tm...  17.8 us
    all_gather x1, blocking collectives, local(): edges = lax.all_gather(facing, 'tm', axis_index_groups=pairs)  13 us
    all_to_all x1, blocking collectives, local(): lax.all_to_all(extended, 'tm', 0, 0, axis_index_groups=quads, tiled=True)  11.7 us
    pallas_call x1, Pallas kernels, correlate(): pl.pallas_call(correlate_kernel, out_shape=jax.ShapeDtypeStruct((SLOTS, L...  3.29 us

profile of v7, /device:TPU:16, one launch (start us, length us, event | category | flops | bytes accessed | tf_op | source)
XLA Modules:
  0.0 76.2 jit_solution(14961502096766512918)
XLA Ops:
  0.0 0.0 copy-start
  0.0 0.0 copy-start.1
  0.0 1.2 %copy-done.1 = bf16[256,1024]{1,0:T(8,128)(2,1)S(1)} copy-done((bf16[256,1024]{1,0:T(8,128)(2,1)S(1)}, bf16[256,1024]{1,0:T(8,128)(2,1)}, u32[]{:S(2)}) %copy-start.1) | copy-done | bytes 524312
  1.2 0.2 stage.1
  1.3 13.0 %all-gather = bf16[256,128]{1,0:T(8,128)(2,1)S(1)} all-gather(bf16[128,128]{1,0:T(8,128)(2,1)S(1)} %get-tuple-element.7), channel_id=2, replica_groups={{8,16},{24,32},{40,48},{56,64},{72,80},{88,96},{104,112},{120,128},{136..., dimensions={0}, use_global_device_ids=true | all-gather | bytes 98304 | tf_op jit(solution)/shard_map/all_gather | solution.py:303
  14.3 0.1 join.1
  14.4 0.0 copy-start.2
  14.4 11.7 %all_to_all.10.x_ref = bf16[4,544,128]{2,1,0:T(8,128)(2,1)S(1)} all-to-all(bf16[4,544,128]{2,1,0:T(8,128)(2,1)S(1)} %join.1), channel_id=1, replica_groups={{0,8,16,24},{32,40,48,56},{64,72,80,88},{96,104,112,120},{128,136,144,1..., dimensions={0} | all-to-all | bytes 1114112 | tf_op jit(solution)/shard_map/all_to_all | solution.py:315
  26.1 0.0 copy-done
  26.1 0.0 copy-start.3
  26.1 0.0 copy-start.4
  26.1 1.4 %spectra.1 = bf16[384,128]{1,0:T(8,128)(2,1)S(1)} custom-call(bf16[768,1024]{1,0:T(8,128)(2,1)S(1)} %copy-done, bf16[4,544,128]{2,1,0:T(8,128)(2,1)S(1)} %all_to_all.10.x_ref), custom_call_target="tpu_custom_call" | custom-call | tf_op jit(solution)/shard_map/spectra/pallas_call | solution.py:316
  27.4 17.8 %all_to_all.11 = bf16[64,3,2,128]{3,2,1,0:T(2,128)(2,1)S(1)} all-to-all(bf16[64,3,2,128]{3,2,1,0:T(2,128)(2,1)S(1)} %bitcast.9), channel_id=1, replica_groups=mesh['tm'=64,'pairs'=8] {'tm'}, dimensions={0} | all-to-all | bytes 196608 | tf_op jit(solution)/shard_map/all_to_all | solution.py:324
  45.3 0.0 copy-done.2
  45.3 0.5 arrange.1
  45.7 27.2 %all_gather.11.s_ref = bf16[3072,128]{1,0:T(8,128)(2,1)S(1)} all-gather(bf16[384,128]{1,0:T(8,128)(2,1)S(1)} %arrange.1), channel_id=1, replica_groups=mesh['tm'=64,'pairs'=8] {'pairs'}, dimensions={0}, use_global_device_ids=true | all-gather | bytes 884736 | tf_op jit(solution)/shard_map/all_gather | solution.py:335
  72.9 0.0 copy-done.3
  72.9 0.0 copy-done.4
  72.9 3.3 %correlate.1 = bf16[10,6,64,128]{3,2,1,0:T(8,128)(2,1)} custom-call(s32[2,10]{1,0:T(2,128)S(1)} %bitcast.12, s32[2048]{0:T(1024)S(1)} %copy-done.3, bf16[3072,128]{1,0:T(8,128)(2,1)S(1)} %all_gather.11.s_ref), custom_call_target="tpu_custom_call" | custom-call | tf_op jit(solution)/shard_map/correlate/pallas_call | solution.py:268
Async XLA Ops:
  0.0 26.1 %copy-start = (bf16[768,1024]{1,0:T(8,128)(2,1)S(1)}, bf16[768,1024]{1,0:T(8,128)(2,1)}, u32[]{:S(2)}) copy-start(bf16[768,1024]{1,0:T(8,128)(2,1)} %constant.4.clone.table_ref) | copy-start | bytes 4718596
  0.0 1.2 %copy-start.1 = (bf16[256,1024]{1,0:T(8,128)(2,1)S(1)}, bf16[256,1024]{1,0:T(8,128)(2,1)}, u32[]{:S(2)}) copy-start(bf16[256,1024]{1,0:T(8,128)(2,1)} %x_ref.1) | copy-start | bytes 1572868
  14.4 30.9 %copy-start.2 = (bf16[384,384]{1,0:T(8,128)(2,1)S(1)}, bf16[384,384]{1,0:T(8,128)(2,1)}, u32[]{:S(2)}) copy-start(bf16[384,384]{1,0:T(8,128)(2,1)} %constant.5.clone.pick_ref) | copy-start | bytes 884740
  26.1 46.8 %copy-start.3 = (s32[2048]{0:T(1024)S(1)}, s32[2048]{0:T(1024)}, u32[]{:S(2)}) copy-start(s32[2048]{0:T(1024)} %order_any.1) | copy-start | bytes 24580
  26.1 46.8 %copy-start.4 = (s32[10,2]{0,1:T(2,128)S(1)}, s32[10,2]{0,1:T(2,128)}, u32[]{:S(2)}) copy-start(s32[10,2]{0,1:T(2,128)} %param.7) | copy-start | bytes 244

commit v8 on v7

--- a/solution.py
+++ b/solution.py
@@ -48,14 +48,28 @@
 PACKED = PART // 2
 
 
-def stage_kernel(x_ref, facing_ref, out_ref):
+def stage_kernel(x_hbm, facing_ref, out_ref, sems):
     low = lax.broadcasted_iota(jnp.int32, (PACKED, 128), 1) < HALF
+    copies = [
+        pltpu.make_async_copy(
+            x_hbm.at[:, :, c * 128 : (c + 1) * 128],
+            out_ref.at[:, c * PART : (c + 1) * PART],
+            sems.at[c],
+        )
+        for c in range(TILES)
+    ]
+    order = [0, TILES - 1] + list(range(1, TILES - 1))
+    for c in order:
+        copies[c].start()
+    for q in range(QUAD):
+        out_ref[q, BODY:] = jnp.zeros((PACKED, 128), bf16)
+    copies[0].wait()
+    copies[TILES - 1].wait()
 
     def pack(column, first_half):
-        edge = x_ref[:, column : column + 128].astype(f32)
         for q in range(QUAD):
-            a = edge[q * PART : q * PART + PACKED]
-            b = edge[q * PART + PACKED : (q + 1) * PART]
+            edge = out_ref[q, column * PART : (column + 1) * PART].astype(f32)
+            a, b = edge[:PACKED], edge[PACKED:]
             if first_half:
                 b = pltpu.roll(b, HALF, 1)
             else:
@@ -66,18 +80,14 @@
 
     @pl.when(odd)
     def _():
-        pack(SLICE - 128, False)
+        pack(TILES - 1, False)
 
     @pl.when(jnp.logical_not(odd))
     def _():
         pack(0, True)
 
-    for q in range(QUAD):
-        for c in range(TILES):
-            out_ref[q, c * PART : (c + 1) * PART] = x_ref[
-                q * PART : (q + 1) * PART, c * 128 : (c + 1) * 128
-            ]
-        out_ref[q, BODY:] = jnp.zeros((PACKED, 128), bf16)
+    for c in order[2:]:
+        copies[c].wait()
 
 
 def join_kernel(edges_ref, _, out_ref, sems):
@@ -294,11 +304,12 @@
             jax.ShapeDtypeStruct((QUAD * PACKED, 128), bf16),
             jax.ShapeDtypeStruct((QUAD, BODY + PACKED, 128), bf16),
         ],
-        in_specs=[vmem()],
+        in_specs=[pl.BlockSpec(memory_space=pltpu.HBM)],
         out_specs=[vmem()] * 2,
+        scratch_shapes=[pltpu.SemaphoreType.DMA((TILES,))],
         compiler_params=PARAMS,
         name="stage",
-    )(records)
+    )(pltpu.with_memory_space_constraint(records.reshape(QUAD, PART, SLICE), pltpu.HBM))
     pairs = [[i, (i + 1) % N_TIME] for i in range(1, N_TIME, 2)]
     edges = lax.all_gather(facing, "tm", axis_index_groups=pairs)
     extended = pl.pallas_call(

time: 76.4 us -> 76.4 us (level)
  local copies, waits for them, and re-layouts: 1.18 us -> 0.02 us
  Pallas kernels: 5.36 us -> 6.46 us
    unnamed x10 -> x8, local copies, waits for them, and re-layouts: 1.18 us -> 0.02 us
    pallas_call x1, Pallas kernels: 0.18 us -> 1.27 us  [local(): pl.pallas_call(stage_kernel, out_shape=[jax.ShapeDtypeStruct((QUAD * PACK...]
where the time goes in v8:
time: 76.4 us; the launch traced here: 76.2 us
  blocking collectives  69.6 us (91%)
  Pallas kernels  6.46 us (8%)
    all_gather x1, blocking collectives, local(): stations = lax.all_gather(mine, 'pairs', axis=0, tiled=True)  27.2 us
    all_to_all x1, blocking collectives, local(): lax.all_to_all(spectra.reshape(N_TIME, LOCAL_BINS // 2, 2, 2 * PART), 'tm...  17.8 us
    all_gather x1, blocking collectives, local(): edges = lax.all_gather(facing, 'tm', axis_index_groups=pairs)  12.9 us
    all_to_all x1, blocking collectives, local(): lax.all_to_all(extended, 'tm', 0, 0, axis_index_groups=quads, tiled=True)  11.7 us
    pallas_call x1, Pallas kernels, correlate(): pl.pallas_call(correlate_kernel, out_shape=jax.ShapeDtypeStruct((SLOTS, L...  3.3 us

profile of v8, /device:TPU:16, one launch (start us, length us, event | category | flops | bytes accessed | tf_op | source)
XLA Modules:
  0.0 76.2 jit_solution(1289311576666022175)
XLA Ops:
  0.0 0.0 copy-start
  0.0 1.3 %stage.1 = (bf16[128,128]{1,0:T(8,128)(2,1)S(1)}, bf16[4,544,128]{2,1,0:T(8,128)(2,1)S(1)}) custom-call(bf16[4,64,1024]{2,1,0:T(8,128)(2,1)} %bitcast.14), custom_call_target="tpu_custom_call" | custom-call | tf_op jit(solution)/shard_map/stage/pallas_call | solution.py:301
  1.3 12.9 %all-gather = bf16[256,128]{1,0:T(8,128)(2,1)S(1)} all-gather(bf16[128,128]{1,0:T(8,128)(2,1)S(1)} %get-tuple-element.7), channel_id=2, replica_groups={{8,16},{24,32},{40,48},{56,64},{72,80},{88,96},{104,112},{120,128},{136..., dimensions={0}, use_global_device_ids=true | all-gather | bytes 98304 | tf_op jit(solution)/shard_map/all_gather | solution.py:314
  14.2 0.1 join.1
  14.3 0.0 copy-start.1
  14.3 11.7 %all_to_all.10.x_ref = bf16[4,544,128]{2,1,0:T(8,128)(2,1)S(1)} all-to-all(bf16[4,544,128]{2,1,0:T(8,128)(2,1)S(1)} %join.1), channel_id=1, replica_groups={{0,8,16,24},{32,40,48,56},{64,72,80,88},{96,104,112,120},{128,136,144,1..., dimensions={0} | all-to-all | bytes 1114112 | tf_op jit(solution)/shard_map/all_to_all | solution.py:326
  26.0 0.0 copy-done
  26.0 0.0 copy-start.2
  26.0 0.0 copy-start.3
  26.0 1.4 %spectra.1 = bf16[384,128]{1,0:T(8,128)(2,1)S(1)} custom-call(bf16[768,1024]{1,0:T(8,128)(2,1)S(1)} %copy-done, bf16[4,544,128]{2,1,0:T(8,128)(2,1)S(1)} %all_to_all.10.x_ref), custom_call_target="tpu_custom_call" | custom-call | tf_op jit(solution)/shard_map/spectra/pallas_call | solution.py:327
  27.4 17.8 %all_to_all.11 = bf16[64,3,2,128]{3,2,1,0:T(2,128)(2,1)S(1)} all-to-all(bf16[64,3,2,128]{3,2,1,0:T(2,128)(2,1)S(1)} %bitcast.10), channel_id=1, replica_groups=mesh['tm'=64,'pairs'=8] {'tm'}, dimensions={0} | all-to-all | bytes 196608 | tf_op jit(solution)/shard_map/all_to_all | solution.py:335
  45.2 0.0 copy-done.1
  45.2 0.5 arrange.1
  45.7 27.2 %all_gather.11.s_ref = bf16[3072,128]{1,0:T(8,128)(2,1)S(1)} all-gather(bf16[384,128]{1,0:T(8,128)(2,1)S(1)} %arrange.1), channel_id=1, replica_groups=mesh['tm'=64,'pairs'=8] {'pairs'}, dimensions={0}, use_global_device_ids=true | all-gather | bytes 884736 | tf_op jit(solution)/shard_map/all_gather | solution.py:346
  72.9 0.0 copy-done.2
  72.9 0.0 copy-done.3
  72.9 3.3 %correlate.1 = bf16[10,6,64,128]{3,2,1,0:T(8,128)(2,1)} custom-call(s32[2,10]{1,0:T(2,128)S(1)} %bitcast.13, s32[2048]{0:T(1024)S(1)} %copy-done.2, bf16[3072,128]{1,0:T(8,128)(2,1)S(1)} %all_gather.11.s_ref), custom_call_target="tpu_custom_call" | custom-call | tf_op jit(solution)/shard_map/correlate/pallas_call | solution.py:278
Async XLA Ops:
  0.0 26.0 %copy-start = (bf16[768,1024]{1,0:T(8,128)(2,1)S(1)}, bf16[768,1024]{1,0:T(8,128)(2,1)}, u32[]{:S(2)}) copy-start(bf16[768,1024]{1,0:T(8,128)(2,1)} %constant.4.clone.table_ref) | copy-start | bytes 4718596
  14.3 30.9 %copy-start.1 = (bf16[384,384]{1,0:T(8,128)(2,1)S(1)}, bf16[384,384]{1,0:T(8,128)(2,1)}, u32[]{:S(2)}) copy-start(bf16[384,384]{1,0:T(8,128)(2,1)} %constant.5.clone.pick_ref) | copy-start | bytes 884740
  26.0 46.9 %copy-start.2 = (s32[2048]{0:T(1024)S(1)}, s32[2048]{0:T(1024)}, u32[]{:S(2)}) copy-start(s32[2048]{0:T(1024)} %order_any.1) | copy-start | bytes 24580
  26.0 46.9 %copy-start.3 = (s32[10,2]{0,1:T(2,128)S(1)}, s32[10,2]{0,1:T(2,128)}, u32[]{:S(2)}) copy-start(s32[10,2]{0,1:T(2,128)} %param.7) | copy-start | bytes 244

commit v9 on v7

--- a/solution.py
+++ b/solution.py
@@ -332,7 +332,10 @@
         compiler_params=PARAMS,
         name="arrange",
     )(jnp.asarray(bin_rows()), by_bin)
-    stations = lax.all_gather(mine, "pairs", axis=0, tiled=True)
+    twos = [[i, i + 1] for i in range(0, N_OWNER, 2)]
+    fours = [list(range(i, N_OWNER, 2)) for i in range(2)]
+    two = lax.all_gather(mine, "pairs", axis=0, axis_index_groups=twos, tiled=True)
+    stations = lax.all_gather(two, "pairs", axis=0, axis_index_groups=fours, tiled=True)
     out = correlate(block_list, station_order, stations)
     out = out.reshape(SLOTS, LOCAL_BINS, GSIZE // 2, 2, 128)
     return jnp.transpose(out, (0, 1, 3, 2, 4)).reshape(SLOTS, LOCAL_BINS, 2, GSIZE * GSIZE)

time: 76.4 us -> 75.7 us (level)
  the two profiles are of different devices: /device:TPU:16 before, /device:TPU:2 now
where the time goes in v9:
time: 75.7 us; the launch traced here: 75.4 us
  blocking collectives  68.9 us (91%)
  Pallas kernels  5.37 us (7%)
  local copies, waits for them, and re-layouts  1.18 us (2%)
    all_gather x1, blocking collectives, local(): lax.all_gather(two, 'pairs', axis=0, axis_index_groups=fours, tiled=True)  21.9 us
    all_to_all x1, blocking collectives, local(): lax.all_to_all(extended, 'tm', 0, 0, axis_index_groups=quads, tiled=True)  19.5 us
    all_to_all x1, blocking collectives, local(): lax.all_to_all(spectra.reshape(N_TIME, LOCAL_BINS // 2, 2, 2 * PART), 'tm...  17.9 us
    all_gather x1, blocking collectives, local(): lax.all_gather(mine, 'pairs', axis=0, axis_index_groups=twos, tiled=True)  5.49 us
    all_gather x1, blocking collectives, local(): edges = lax.all_gather(facing, 'tm', axis_index_groups=pairs)  4.02 us
    pallas_call x1, Pallas kernels, correlate(): pl.pallas_call(correlate_kernel, out_shape=jax.ShapeDtypeStruct((SLOTS, L...  3.3 us

profile of v9, /device:TPU:2, one launch (start us, length us, event | category | flops | bytes accessed | tf_op | source)
XLA Modules:
  0.0 75.4 jit_solution(6143060839526879055)
XLA Ops:
  0.0 0.0 copy-start
  0.0 0.0 copy-start.1
  0.0 1.2 %copy-done.1 = bf16[256,1024]{1,0:T(8,128)(2,1)S(1)} copy-done((bf16[256,1024]{1,0:T(8,128)(2,1)S(1)}, bf16[256,1024]{1,0:T(8,128)(2,1)}, u32[]{:S(2)}) %copy-start.1) | copy-done | bytes 524312
  1.2 0.2 stage.1
  1.3 4.0 %all-gather = bf16[256,128]{1,0:T(8,128)(2,1)S(1)} all-gather(bf16[128,128]{1,0:T(8,128)(2,1)S(1)} %get-tuple-element.7), channel_id=2, replica_groups={{8,16},{24,32},{40,48},{56,64},{72,80},{88,96},{104,112},{120,128},{136..., dimensions={0}, use_global_device_ids=true | all-gather | bytes 98304 | tf_op jit(solution)/shard_map/all_gather | solution.py:303
  5.4 0.1 join.1
  5.4 0.0 copy-start.2
  5.4 19.5 %all_to_all.10.x_ref = bf16[4,544,128]{2,1,0:T(8,128)(2,1)S(1)} all-to-all(bf16[4,544,128]{2,1,0:T(8,128)(2,1)S(1)} %join.1), channel_id=1, replica_groups={{0,8,16,24},{32,40,48,56},{64,72,80,88},{96,104,112,120},{128,136,144,1..., dimensions={0} | all-to-all | bytes 1114112 | tf_op jit(solution)/shard_map/all_to_all | solution.py:315
  24.9 0.0 copy-done
  24.9 0.0 copy-start.3
  25.0 0.0 copy-start.4
  25.0 1.4 %spectra.1 = bf16[384,128]{1,0:T(8,128)(2,1)S(1)} custom-call(bf16[768,1024]{1,0:T(8,128)(2,1)S(1)} %copy-done, bf16[4,544,128]{2,1,0:T(8,128)(2,1)S(1)} %all_to_all.10.x_ref), custom_call_target="tpu_custom_call" | custom-call | tf_op jit(solution)/shard_map/spectra/pallas_call | solution.py:316
  26.3 17.9 %all_to_all.11 = bf16[64,3,2,128]{3,2,1,0:T(2,128)(2,1)S(1)} all-to-all(bf16[64,3,2,128]{3,2,1,0:T(2,128)(2,1)S(1)} %bitcast.9), channel_id=1, replica_groups=mesh['tm'=64,'pairs'=8] {'tm'}, dimensions={0} | all-to-all | bytes 196608 | tf_op jit(solution)/shard_map/all_to_all | solution.py:324
  44.3 0.0 copy-done.2
  44.3 0.5 arrange.1
  44.7 5.5 %all_gather.14 = bf16[768,128]{1,0:T(8,128)(2,1)S(1)} all-gather(bf16[384,128]{1,0:T(8,128)(2,1)S(1)} %arrange.1), channel_id=1, replica_groups={{0,1},{2,3},{4,5},{6,7},{8,9},{10,11},{12,13},{14,15},{16,17},{18,19},{..., dimensions={0}, use_global_device_ids=true | all-gather | bytes 294912 | tf_op jit(solution)/shard_map/all_gather | solution.py:337
  50.2 21.9 %all_gather.15.s_ref = bf16[3072,128]{1,0:T(8,128)(2,1)S(1)} all-gather(bf16[768,128]{1,0:T(8,128)(2,1)S(1)} %all_gather.14), channel_id=1, replica_groups={{0,2,4,6},{1,3,5,7},{8,10,12,14},{9,11,13,15},{16,18,20,22},{17,19,21,2..., dimensions={0}, use_global_device_ids=true | all-gather | bytes 983040 | tf_op jit(solution)/shard_map/all_gather | solution.py:338
  72.1 0.0 copy-done.3
  72.1 0.0 copy-done.4
  72.1 3.3 %correlate.1 = bf16[10,6,64,128]{3,2,1,0:T(8,128)(2,1)} custom-call(s32[2,10]{1,0:T(2,128)S(1)} %bitcast.12, s32[2048]{0:T(1024)S(1)} %copy-done.3, bf16[3072,128]{1,0:T(8,128)(2,1)S(1)} %all_gather.15.s_ref), custom_call_target="tpu_custom_call" | custom-call | tf_op jit(solution)/shard_map/correlate/pallas_call | solution.py:268
Async XLA Ops:
  0.0 24.9 %copy-start = (bf16[768,1024]{1,0:T(8,128)(2,1)S(1)}, bf16[768,1024]{1,0:T(8,128)(2,1)}, u32[]{:S(2)}) copy-start(bf16[768,1024]{1,0:T(8,128)(2,1)} %constant.4.clone.table_ref) | copy-start | bytes 4718596
  0.0 1.2 %copy-start.1 = (bf16[256,1024]{1,0:T(8,128)(2,1)S(1)}, bf16[256,1024]{1,0:T(8,128)(2,1)}, u32[]{:S(2)}) copy-start(bf16[256,1024]{1,0:T(8,128)(2,1)} %x_ref.1) | copy-start | bytes 1572868
  5.4 38.8 %copy-start.2 = (bf16[384,384]{1,0:T(8,128)(2,1)S(1)}, bf16[384,384]{1,0:T(8,128)(2,1)}, u32[]{:S(2)}) copy-start(bf16[384,384]{1,0:T(8,128)(2,1)} %constant.5.clone.pick_ref) | copy-start | bytes 884740
  24.9 47.2 %copy-start.3 = (s32[2048]{0:T(1024)S(1)}, s32[2048]{0:T(1024)}, u32[]{:S(2)}) copy-start(s32[2048]{0:T(1024)} %order_any.1) | copy-start | bytes 24580
  25.0 47.2 %copy-start.4 = (s32[10,2]{0,1:T(2,128)S(1)}, s32[10,2]{0,1:T(2,128)}, u32[]{:S(2)}) copy-start(s32[10,2]{0,1:T(2,128)} %param.7) | copy-start | bytes 244

commit v10 on v9

--- a/solution.py
+++ b/solution.py
@@ -271,8 +271,8 @@
         in_specs=[pl.BlockSpec(memory_space=pl.ANY), pl.BlockSpec(memory_space=pl.ANY), vmem()],
         out_specs=pl.BlockSpec(memory_space=pltpu.HBM),
         scratch_shapes=[
-            pltpu.VMEM((RECEIVER_TOTAL, 128), f32),
-            pltpu.VMEM((RECEIVER_TOTAL, 128), f32),
+            pltpu.VMEM((RECEIVER_TOTAL + 8, 128), f32),
+            pltpu.VMEM((RECEIVER_TOTAL + 8, 128), f32),
             pltpu.VMEM((SLOTS * 3 * GSIZE, 128), f32),
             pltpu.VMEM((SLOTS * 3 * GSIZE, 128), f32),
             pltpu.VMEM((SLOTS, LOCAL_BINS, GSIZE, 128), bf16),

time: 75.7 us -> 75.6 us (level)
  no operation moved by 1% of the time
where the time goes in v10:
time: 75.6 us; the launch traced here: 75.4 us
  blocking collectives  68.9 us (91%)
  Pallas kernels  5.36 us (7%)
  local copies, waits for them, and re-layouts  1.18 us (2%)
    all_gather x1, blocking collectives, local(): lax.all_gather(two, 'pairs', axis=0, axis_index_groups=fours, tiled=True)  21.9 us
    all_to_all x1, blocking collectives, local(): lax.all_to_all(extended, 'tm', 0, 0, axis_index_groups=quads, tiled=True)  19.5 us
    all_to_all x1, blocking collectives, local(): lax.all_to_all(spectra.reshape(N_TIME, LOCAL_BINS // 2, 2, 2 * PART), 'tm...  17.9 us
    all_gather x1, blocking collectives, local(): lax.all_gather(mine, 'pairs', axis=0, axis_index_groups=twos, tiled=True)  5.49 us
    all_gather x1, blocking collectives, local(): edges = lax.all_gather(facing, 'tm', axis_index_groups=pairs)  4.02 us
    pallas_call x1, Pallas kernels, correlate(): pl.pallas_call(correlate_kernel, out_shape=jax.ShapeDtypeStruct((SLOTS, L...  3.29 us

profile of v10, /device:TPU:2, one launch (start us, length us, event | category | flops | bytes accessed | tf_op | source)
XLA Modules:
  0.0 75.4 jit_solution(9069348875293608849)
XLA Ops:
  0.0 0.0 copy-start
  0.0 0.0 copy-start.1
  0.0 1.2 %copy-done.1 = bf16[256,1024]{1,0:T(8,128)(2,1)S(1)} copy-done((bf16[256,1024]{1,0:T(8,128)(2,1)S(1)}, bf16[256,1024]{1,0:T(8,128)(2,1)}, u32[]{:S(2)}) %copy-start.1) | copy-done | bytes 524312
  1.2 0.2 stage.1
  1.3 4.0 %all-gather = bf16[256,128]{1,0:T(8,128)(2,1)S(1)} all-gather(bf16[128,128]{1,0:T(8,128)(2,1)S(1)} %get-tuple-element.7), channel_id=2, replica_groups={{8,16},{24,32},{40,48},{56,64},{72,80},{88,96},{104,112},{120,128},{136..., dimensions={0}, use_global_device_ids=true | all-gather | bytes 98304 | tf_op jit(solution)/shard_map/all_gather | solution.py:303
  5.4 0.1 join.1
  5.4 0.0 copy-start.2
  5.4 19.5 %all_to_all.10.x_ref = bf16[4,544,128]{2,1,0:T(8,128)(2,1)S(1)} all-to-all(bf16[4,544,128]{2,1,0:T(8,128)(2,1)S(1)} %join.1), channel_id=1, replica_groups={{0,8,16,24},{32,40,48,56},{64,72,80,88},{96,104,112,120},{128,136,144,1..., dimensions={0} | all-to-all | bytes 1114112 | tf_op jit(solution)/shard_map/all_to_all | solution.py:315
  24.9 0.0 copy-done
  24.9 0.0 copy-start.3
  25.0 0.0 copy-start.4
  25.0 1.4 %spectra.1 = bf16[384,128]{1,0:T(8,128)(2,1)S(1)} custom-call(bf16[768,1024]{1,0:T(8,128)(2,1)S(1)} %copy-done, bf16[4,544,128]{2,1,0:T(8,128)(2,1)S(1)} %all_to_all.10.x_ref), custom_call_target="tpu_custom_call" | custom-call | tf_op jit(solution)/shard_map/spectra/pallas_call | solution.py:316
  26.3 17.9 %all_to_all.11 = bf16[64,3,2,128]{3,2,1,0:T(2,128)(2,1)S(1)} all-to-all(bf16[64,3,2,128]{3,2,1,0:T(2,128)(2,1)S(1)} %bitcast.9), channel_id=1, replica_groups=mesh['tm'=64,'pairs'=8] {'tm'}, dimensions={0} | all-to-all | bytes 196608 | tf_op jit(solution)/shard_map/all_to_all | solution.py:324
  44.3 0.0 copy-done.2
  44.3 0.5 arrange.1
  44.7 5.5 %all_gather.14 = bf16[768,128]{1,0:T(8,128)(2,1)S(1)} all-gather(bf16[384,128]{1,0:T(8,128)(2,1)S(1)} %arrange.1), channel_id=1, replica_groups={{0,1},{2,3},{4,5},{6,7},{8,9},{10,11},{12,13},{14,15},{16,17},{18,19},{..., dimensions={0}, use_global_device_ids=true | all-gather | bytes 294912 | tf_op jit(solution)/shard_map/all_gather | solution.py:337
  50.2 21.9 %all_gather.15.s_ref = bf16[3072,128]{1,0:T(8,128)(2,1)S(1)} all-gather(bf16[768,128]{1,0:T(8,128)(2,1)S(1)} %all_gather.14), channel_id=1, replica_groups={{0,2,4,6},{1,3,5,7},{8,10,12,14},{9,11,13,15},{16,18,20,22},{17,19,21,2..., dimensions={0}, use_global_device_ids=true | all-gather | bytes 983040 | tf_op jit(solution)/shard_map/all_gather | solution.py:338
  72.1 0.0 copy-done.3
  72.1 0.0 copy-done.4
  72.1 3.3 %correlate.1 = bf16[10,6,64,128]{3,2,1,0:T(8,128)(2,1)} custom-call(s32[2,10]{1,0:T(2,128)S(1)} %bitcast.12, s32[2048]{0:T(1024)S(1)} %copy-done.3, bf16[3072,128]{1,0:T(8,128)(2,1)S(1)} %all_gather.15.s_ref), custom_call_target="tpu_custom_call" | custom-call | tf_op jit(solution)/shard_map/correlate/pallas_call | solution.py:268
Async XLA Ops:
  0.0 24.9 %copy-start = (bf16[768,1024]{1,0:T(8,128)(2,1)S(1)}, bf16[768,1024]{1,0:T(8,128)(2,1)}, u32[]{:S(2)}) copy-start(bf16[768,1024]{1,0:T(8,128)(2,1)} %constant.4.clone.table_ref) | copy-start | bytes 4718596
  0.0 1.2 %copy-start.1 = (bf16[256,1024]{1,0:T(8,128)(2,1)S(1)}, bf16[256,1024]{1,0:T(8,128)(2,1)}, u32[]{:S(2)}) copy-start(bf16[256,1024]{1,0:T(8,128)(2,1)} %x_ref.1) | copy-start | bytes 1572868
  5.4 38.8 %copy-start.2 = (bf16[384,384]{1,0:T(8,128)(2,1)S(1)}, bf16[384,384]{1,0:T(8,128)(2,1)}, u32[]{:S(2)}) copy-start(bf16[384,384]{1,0:T(8,128)(2,1)} %constant.5.clone.pick_ref) | copy-start | bytes 884740
  24.9 47.2 %copy-start.3 = (s32[2048]{0:T(1024)S(1)}, s32[2048]{0:T(1024)}, u32[]{:S(2)}) copy-start(s32[2048]{0:T(1024)} %order_any.1) | copy-start | bytes 24580
  25.0 47.2 %copy-start.4 = (s32[10,2]{0,1:T(2,128)S(1)}, s32[10,2]{0,1:T(2,128)}, u32[]{:S(2)}) copy-start(s32[10,2]{0,1:T(2,128)} %param.7) | copy-start | bytes 244

commit v11 on v8

--- a/solution.py
+++ b/solution.py
@@ -133,15 +133,27 @@
     return jnp.concatenate(blocks, axis=1)
 
 
-def spectra_kernel(table_ref, x_ref, out_ref):
+def spectra_kernel(table_hbm, x_ref, out_ref, table_ref, sems):
+    loads = [
+        pltpu.make_async_copy(
+            table_hbm.at[c * BINS : (c + 1) * BINS],
+            table_ref.at[c * BINS : (c + 1) * BINS],
+            sems.at[c],
+        )
+        for c in range(2)
+    ]
+    for load in loads:
+        load.start()
     columns = [
         jnp.concatenate([x_ref[q, c * PART : (c + 1) * PART] for q in range(QUAD)], axis=0)
         for c in range(TILES)
     ]
     x = jnp.concatenate(columns, axis=1)
     y = normalize(lax.axis_index("tm") // QUAD, x, x_ref[0, BODY:], x_ref[QUAD - 1, BODY:])
-    p = lax.dot_general(table_ref[...], y, NT, preferred_element_type=f32)
-    re, im = p[:BINS], p[BINS:]
+    loads[0].wait()
+    re = lax.dot_general(table_ref[:BINS], y, NT, preferred_element_type=f32)
+    loads[1].wait()
+    im = lax.dot_general(table_ref[BINS:], y, NT, preferred_element_type=f32)
     f = lax.broadcasted_iota(jnp.int32, (BINS, 128), 0)
     lane = lax.broadcasted_iota(jnp.int32, (BINS, 128), 1)
     odd = (f & 1) == 1
@@ -281,8 +293,8 @@
         in_specs=[pl.BlockSpec(memory_space=pl.ANY), pl.BlockSpec(memory_space=pl.ANY), vmem()],
         out_specs=pl.BlockSpec(memory_space=pltpu.HBM),
         scratch_shapes=[
-            pltpu.VMEM((RECEIVER_TOTAL, 128), f32),
-            pltpu.VMEM((RECEIVER_TOTAL, 128), f32),
+            pltpu.VMEM((RECEIVER_TOTAL + 8, 128), f32),
+            pltpu.VMEM((RECEIVER_TOTAL + 8, 128), f32),
             pltpu.VMEM((SLOTS * 3 * GSIZE, 128), f32),
             pltpu.VMEM((SLOTS * 3 * GSIZE, 128), f32),
             pltpu.VMEM((SLOTS, LOCAL_BINS, GSIZE, 128), bf16),
@@ -327,11 +339,15 @@
     spectra = pl.pallas_call(
         spectra_kernel,
         out_shape=jax.ShapeDtypeStruct((BINS, 2 * PART), bf16),
-        in_specs=[vmem(), vmem()],
+        in_specs=[pl.BlockSpec(memory_space=pltpu.HBM), vmem()],
         out_specs=vmem(),
+        scratch_shapes=[
+            pltpu.VMEM((2 * BINS, SLICE), bf16),
+            pltpu.SemaphoreType.DMA((2,)),
+        ],
         compiler_params=PARAMS,
         name="spectra",
-    )(jnp.asarray(quarter_table()), windows)
+    )(pltpu.with_memory_space_constraint(jnp.asarray(quarter_table()), pltpu.HBM), windows)
     by_bin = lax.all_to_all(
         spectra.reshape(N_TIME, LOCAL_BINS // 2, 2, 2 * PART), "tm", 0, 0, tiled=True
     ).reshape(BINS, 2 * PART)
@@ -343,7 +359,10 @@
         compiler_params=PARAMS,
         name="arrange",
     )(jnp.asarray(bin_rows()), by_bin)
-    stations = lax.all_gather(mine, "pairs", axis=0, tiled=True)
+    twos = [[i, i + 1] for i in range(0, N_OWNER, 2)]
+    fours = [list(range(i, N_OWNER, 2)) for i in range(2)]
+    two = lax.all_gather(mine, "pairs", axis=0, axis_index_groups=twos, tiled=True)
+    stations = lax.all_gather(two, "pairs", axis=0, axis_index_groups=fours, tiled=True)
     out = correlate(block_list, station_order, stations)
     out = out.reshape(SLOTS, LOCAL_BINS, GSIZE // 2, 2, 128)
     return jnp.transpose(out, (0, 1, 3, 2, 4)).reshape(SLOTS, LOCAL_BINS, 2, GSIZE * GSIZE)

time: 76.4 us -> 76.7 us (level)
  the two profiles are of different devices: /device:TPU:16 before, /device:TPU:2 now
where the time goes in v11:
time: 76.7 us; the launch traced here: 76.4 us
  blocking collectives  68.9 us (90%)
  Pallas kernels  7.5 us (10%)
    all_gather x1, blocking collectives, local(): lax.all_gather(two, 'pairs', axis=0, axis_index_groups=fours, tiled=True)  21.9 us
    all_to_all x1, blocking collectives, local(): lax.all_to_all(extended, 'tm', 0, 0, axis_index_groups=quads, tiled=True)  19.5 us
    all_to_all x1, blocking collectives, local(): lax.all_to_all(spectra.reshape(N_TIME, LOCAL_BINS // 2, 2, 2 * PART), 'tm...  17.9 us
    all_gather x1, blocking collectives, local(): lax.all_gather(mine, 'pairs', axis=0, axis_index_groups=twos, tiled=True)  5.49 us
    all_gather x1, blocking collectives, local(): edges = lax.all_gather(facing, 'tm', axis_index_groups=pairs)  4.02 us
    pallas_call x1, Pallas kernels, correlate(): pl.pallas_call(correlate_kernel, out_shape=jax.ShapeDtypeStruct((SLOTS, L...  3.29 us
    pallas_call x1, Pallas kernels, local(): pl.pallas_call(spectra_kernel, out_shape=jax.ShapeDtypeStruct((BINS, 2 *...  2.53 us

profile of v11, /device:TPU:2, one launch (start us, length us, event | category | flops | bytes accessed | tf_op | source)
XLA Modules:
  0.0 76.4 jit_solution(9648043846833206112)
XLA Ops:
  0.0 1.1 %stage.1 = (bf16[128,128]{1,0:T(8,128)(2,1)S(1)}, bf16[4,544,128]{2,1,0:T(8,128)(2,1)S(1)}) custom-call(bf16[4,64,1024]{2,1,0:T(8,128)(2,1)} %bitcast.14), custom_call_target="tpu_custom_call" | custom-call | tf_op jit(solution)/shard_map/stage/pallas_call | solution.py:313
  1.2 4.0 %all-gather = bf16[256,128]{1,0:T(8,128)(2,1)S(1)} all-gather(bf16[128,128]{1,0:T(8,128)(2,1)S(1)} %get-tuple-element.7), channel_id=2, replica_groups={{8,16},{24,32},{40,48},{56,64},{72,80},{88,96},{104,112},{120,128},{136..., dimensions={0}, use_global_device_ids=true | all-gather | bytes 98304 | tf_op jit(solution)/shard_map/all_gather | solution.py:326
  5.2 0.1 join.1
  5.2 0.0 copy-start
  5.3 19.5 %all_to_all.10.x_ref = bf16[4,544,128]{2,1,0:T(8,128)(2,1)S(1)} all-to-all(bf16[4,544,128]{2,1,0:T(8,128)(2,1)S(1)} %join.1), channel_id=1, replica_groups={{0,8,16,24},{32,40,48,56},{64,72,80,88},{96,104,112,120},{128,136,144,1..., dimensions={0} | all-to-all | bytes 1114112 | tf_op jit(solution)/shard_map/all_to_all | solution.py:338
  24.8 0.0 copy-start.1
  24.8 0.0 copy-start.2
  24.8 2.5 %spectra.1 = bf16[384,128]{1,0:T(8,128)(2,1)S(1)} custom-call(bf16[768,1024]{1,0:T(8,128)(2,1)} %constant.4.clone.table_hbm, bf16[4,544,128]{2,1,0:T(8,128)(2,1)S(1)} %all_to_all.10.x_ref), custom_call_target="tpu_custom_call" | custom-call | tf_op jit(solution)/shard_map/spectra/pallas_call | solution.py:339
  27.3 17.9 %all_to_all.11 = bf16[64,3,2,128]{3,2,1,0:T(2,128)(2,1)S(1)} all-to-all(bf16[64,3,2,128]{3,2,1,0:T(2,128)(2,1)S(1)} %bitcast.10), channel_id=1, replica_groups=mesh['tm'=64,'pairs'=8] {'tm'}, dimensions={0} | all-to-all | bytes 196608 | tf_op jit(solution)/shard_map/all_to_all | solution.py:351
  45.2 0.0 copy-done
  45.2 0.5 arrange.1
  45.7 5.5 %all_gather.14 = bf16[768,128]{1,0:T(8,128)(2,1)S(1)} all-gather(bf16[384,128]{1,0:T(8,128)(2,1)S(1)} %arrange.1), channel_id=1, replica_groups={{0,1},{2,3},{4,5},{6,7},{8,9},{10,11},{12,13},{14,15},{16,17},{18,19},{..., dimensions={0}, use_global_device_ids=true | all-gather | bytes 294912 | tf_op jit(solution)/shard_map/all_gather | solution.py:364
  51.2 21.9 %all_gather.15.s_ref = bf16[3072,128]{1,0:T(8,128)(2,1)S(1)} all-gather(bf16[768,128]{1,0:T(8,128)(2,1)S(1)} %all_gather.14), channel_id=1, replica_groups={{0,2,4,6},{1,3,5,7},{8,10,12,14},{9,11,13,15},{16,18,20,22},{17,19,21,2..., dimensions={0}, use_global_device_ids=true | all-gather | bytes 983040 | tf_op jit(solution)/shard_map/all_gather | solution.py:365
  73.1 0.0 copy-done.1
  73.1 0.0 copy-done.2
  73.1 3.3 %correlate.1 = bf16[10,6,64,128]{3,2,1,0:T(8,128)(2,1)} custom-call(s32[2,10]{1,0:T(2,128)S(1)} %bitcast.13, s32[2048]{0:T(1024)S(1)} %copy-done.1, bf16[3072,128]{1,0:T(8,128)(2,1)S(1)} %all_gather.15.s_ref), custom_call_target="tpu_custom_call" | custom-call | tf_op jit(solution)/shard_map/correlate/pallas_call | solution.py:290
Async XLA Ops:
  5.2 40.0 %copy-start = (bf16[384,384]{1,0:T(8,128)(2,1)S(1)}, bf16[384,384]{1,0:T(8,128)(2,1)}, u32[]{:S(2)}) copy-start(bf16[384,384]{1,0:T(8,128)(2,1)} %constant.5.clone.pick_ref) | copy-start | bytes 884740
  24.8 48.4 %copy-start.1 = (s32[2048]{0:T(1024)S(1)}, s32[2048]{0:T(1024)}, u32[]{:S(2)}) copy-start(s32[2048]{0:T(1024)} %order_any.1) | copy-start | bytes 24580
  24.8 48.4 %copy-start.2 = (s32[10,2]{0,1:T(2,128)S(1)}, s32[10,2]{0,1:T(2,128)}, u32[]{:S(2)}) copy-start(s32[10,2]{0,1:T(2,128)} %param.7) | copy-start | bytes 244

commit v12 on v10

--- a/solution.py
+++ b/solution.py
@@ -194,7 +194,8 @@
     list_copy = pltpu.make_async_copy(list_any, list_ref, list_sem)
     list_copy.start()
     for n in range(N_OWNER):
-        block = s_ref[n * BINS : (n + 1) * BINS].astype(f32)
+        at = n // 2 + n % 2 * (N_OWNER // 2)
+        block = s_ref[at * BINS : (at + 1) * BINS].astype(f32)
         main_ref[n * ROWS : (n + 1) * ROWS] = block[:ROWS]
         tail_ref[n * ROWS : n * ROWS + 128] = block[ROWS:]
         tail_ref[n * ROWS + 128 : (n + 1) * ROWS] = pltpu.roll(block[ROWS:], 64, 1)
@@ -334,8 +335,8 @@
     )(jnp.asarray(bin_rows()), by_bin)
     twos = [[i, i + 1] for i in range(0, N_OWNER, 2)]
     fours = [list(range(i, N_OWNER, 2)) for i in range(2)]
-    two = lax.all_gather(mine, "pairs", axis=0, axis_index_groups=twos, tiled=True)
-    stations = lax.all_gather(two, "pairs", axis=0, axis_index_groups=fours, tiled=True)
+    four = lax.all_gather(mine, "pairs", axis=0, axis_index_groups=fours, tiled=True)
+    stations = lax.all_gather(four, "pairs", axis=0, axis_index_groups=twos, tiled=True)
     out = correlate(block_list, station_order, stations)
     out = out.reshape(SLOTS, LOCAL_BINS, GSIZE // 2, 2, 128)
     return jnp.transpose(out, (0, 1, 3, 2, 4)).reshape(SLOTS, LOCAL_BINS, 2, GSIZE * GSIZE)

time: 75.6 us -> 75.7 us (level)
  the two profiles are of different devices: /device:TPU:2 before, /device:TPU:8 now
where the time goes in v12:
time: 75.7 us; the launch traced here: 75.4 us
  blocking collectives  68.8 us (91%)
  Pallas kernels  5.36 us (7%)
  local copies, waits for them, and re-layouts  1.18 us (2%)
    all_to_all x1, blocking collectives, local(): lax.all_to_all(spectra.reshape(N_TIME, LOCAL_BINS // 2, 2, 2 * PART), 'tm...  17.8 us
    all_gather x1, blocking collectives, local(): lax.all_gather(mine, 'pairs', axis=0, axis_index_groups=fours, tiled=True)  17.1 us
    all_gather x1, blocking collectives, local(): edges = lax.all_gather(facing, 'tm', axis_index_groups=pairs)  13 us
    all_to_all x1, blocking collectives, local(): lax.all_to_all(extended, 'tm', 0, 0, axis_index_groups=quads, tiled=True)  11.7 us
    all_gather x1, blocking collectives, local(): lax.all_gather(four, 'pairs', axis=0, axis_index_groups=twos, tiled=True)  9.3 us
    pallas_call x1, Pallas kernels, correlate(): pl.pallas_call(correlate_kernel, out_shape=jax.ShapeDtypeStruct((SLOTS, L...  3.3 us

profile of v12, /device:TPU:8, one launch (start us, length us, event | category | flops | bytes accessed | tf_op | source)
XLA Modules:
  0.0 75.4 jit_solution(8060305796584443981)
XLA Ops:
  0.0 0.0 copy-start
  0.0 0.0 copy-start.1
  0.0 1.2 %copy-done.1 = bf16[256,1024]{1,0:T(8,128)(2,1)S(1)} copy-done((bf16[256,1024]{1,0:T(8,128)(2,1)S(1)}, bf16[256,1024]{1,0:T(8,128)(2,1)}, u32[]{:S(2)}) %copy-start.1) | copy-done | bytes 524312
  1.2 0.2 stage.1
  1.3 13.0 %all-gather = bf16[256,128]{1,0:T(8,128)(2,1)S(1)} all-gather(bf16[128,128]{1,0:T(8,128)(2,1)S(1)} %get-tuple-element.7), channel_id=2, replica_groups={{8,16},{24,32},{40,48},{56,64},{72,80},{88,96},{104,112},{120,128},{136..., dimensions={0}, use_global_device_ids=true | all-gather | bytes 98304 | tf_op jit(solution)/shard_map/all_gather | solution.py:304
  14.3 0.1 join.1
  14.4 0.0 copy-start.2
  14.4 11.7 %all_to_all.10.x_ref = bf16[4,544,128]{2,1,0:T(8,128)(2,1)S(1)} all-to-all(bf16[4,544,128]{2,1,0:T(8,128)(2,1)S(1)} %join.1), channel_id=1, replica_groups={{0,8,16,24},{32,40,48,56},{64,72,80,88},{96,104,112,120},{128,136,144,1..., dimensions={0} | all-to-all | bytes 1114112 | tf_op jit(solution)/shard_map/all_to_all | solution.py:316
  26.1 0.0 copy-done
  26.1 1.4 %spectra.1 = bf16[384,128]{1,0:T(8,128)(2,1)S(1)} custom-call(bf16[768,1024]{1,0:T(8,128)(2,1)S(1)} %copy-done, bf16[4,544,128]{2,1,0:T(8,128)(2,1)S(1)} %all_to_all.10.x_ref), custom_call_target="tpu_custom_call" | custom-call | tf_op jit(solution)/shard_map/spectra/pallas_call | solution.py:317
  27.4 0.0 copy-start.3
  27.5 0.0 copy-start.4
  27.5 17.8 %all_to_all.11 = bf16[64,3,2,128]{3,2,1,0:T(2,128)(2,1)S(1)} all-to-all(bf16[64,3,2,128]{3,2,1,0:T(2,128)(2,1)S(1)} %bitcast.9), channel_id=1, replica_groups=mesh['tm'=64,'pairs'=8] {'tm'}, dimensions={0} | all-to-all | bytes 196608 | tf_op jit(solution)/shard_map/all_to_all | solution.py:325
  45.3 0.0 copy-done.2
  45.3 0.5 arrange.1
  45.8 17.1 %all_gather.14 = bf16[1536,128]{1,0:T(8,128)(2,1)S(1)} all-gather(bf16[384,128]{1,0:T(8,128)(2,1)S(1)} %arrange.1), channel_id=1, replica_groups={{0,2,4,6},{1,3,5,7},{8,10,12,14},{9,11,13,15},{16,18,20,22},{17,19,21,2..., dimensions={0}, use_global_device_ids=true | all-gather | bytes 491520 | tf_op jit(solution)/shard_map/all_gather | solution.py:338
  62.8 9.3 %all_gather.15.s_ref = bf16[3072,128]{1,0:T(8,128)(2,1)S(1)} all-gather(bf16[1536,128]{1,0:T(8,128)(2,1)S(1)} %all_gather.14), channel_id=1, replica_groups={{0,1},{2,3},{4,5},{6,7},{8,9},{10,11},{12,13},{14,15},{16,17},{18,19},{..., dimensions={0}, use_global_device_ids=true | all-gather | bytes 1179648 | tf_op jit(solution)/shard_map/all_gather | solution.py:339
  72.1 0.0 copy-done.3
  72.1 0.0 copy-done.4
  72.1 3.3 %correlate.1 = bf16[10,6,64,128]{3,2,1,0:T(8,128)(2,1)} custom-call(s32[2,10]{1,0:T(2,128)S(1)} %bitcast.12, s32[2048]{0:T(1024)S(1)} %copy-done.3, bf16[3072,128]{1,0:T(8,128)(2,1)S(1)} %all_gather.15.s_ref), custom_call_target="tpu_custom_call" | custom-call | tf_op jit(solution)/shard_map/correlate/pallas_call | solution.py:269
Async XLA Ops:
  0.0 26.1 %copy-start = (bf16[768,1024]{1,0:T(8,128)(2,1)S(1)}, bf16[768,1024]{1,0:T(8,128)(2,1)}, u32[]{:S(2)}) copy-start(bf16[768,1024]{1,0:T(8,128)(2,1)} %constant.4.clone.table_ref) | copy-start | bytes 4718596
  0.0 1.2 %copy-start.1 = (bf16[256,1024]{1,0:T(8,128)(2,1)S(1)}, bf16[256,1024]{1,0:T(8,128)(2,1)}, u32[]{:S(2)}) copy-start(bf16[256,1024]{1,0:T(8,128)(2,1)} %x_ref.1) | copy-start | bytes 1572868
  14.4 30.9 %copy-start.2 = (bf16[384,384]{1,0:T(8,128)(2,1)S(1)}, bf16[384,384]{1,0:T(8,128)(2,1)}, u32[]{:S(2)}) copy-start(bf16[384,384]{1,0:T(8,128)(2,1)} %constant.5.clone.pick_ref) | copy-start | bytes 884740
  27.4 44.7 %copy-start.3 = (s32[2048]{0:T(1024)S(1)}, s32[2048]{0:T(1024)}, u32[]{:S(2)}) copy-start(s32[2048]{0:T(1024)} %order_any.1) | copy-start | bytes 24580
  27.5 44.7 %copy-start.4 = (s32[10,2]{0,1:T(2,128)S(1)}, s32[10,2]{0,1:T(2,128)}, u32[]{:S(2)}) copy-start(s32[10,2]{0,1:T(2,128)} %param.7) | copy-start | bytes 244
